TPU v7x, 768 devices: a whole 4x8x12 slice. The times are simulated.
768 devices in a mesh: gx: 12 (over z), gy: 64 (over y, x, core).
Axes of the slice: x: 4, y: 8, z: 12, core: 2. Of those that a mesh axis runs over, the one named last changes fastest.
Arguments:
- temps: float32 [2, 384, 768, 128], P(None, 'gx', 'gy'), may hold values from 0.5 to 2
- right_side: float32 [2, 384, 768, 128], P(None, 'gx', 'gy'), may hold values from -5 to 5
- exchange: float32 [384, 768, 128], P('gx', 'gy'), may hold values from 0.1 to 1
- coupling: float32 [384, 768, 128], P('gx', 'gy'), may hold values from 0.05 to 0.5
Outputs:
- fields: float32 [2, 384, 768, 128], P(None, 'gx', 'gy')
All inputs are finite; a program needn't handle non-finite values.
Results may differ from a plain program's by a relative error of at most 0.000027.
Values sent between devices are 32-bit elements; how exact they have to be, the bound alone decides.
A program may use at most 64 MiB of HBM per device.

v0:
```python
import jax
import jax.numpy as jnp
from jax import lax
from jax.sharding import PartitionSpec as P

SWEEPS = 2


solid_cap = 0.5
gas_cap = 0.02
flow_rate = 40.0
gas_conduct = 0.05
axis_weights = (1.0, 1.0, 1.0, 1.0, 0.25, 0.25)
relaxation = 0.8
lump_factor = 0.25


def padded_2(x, sides, width):
    for axis, dim in sides:
        count, length = (lax.axis_size(axis), x.shape[dim])
        up = [(i, (i + 1) % count) for i in range(count - 1)]
        down = [(j, i) for i, j in up]
        last = lax.slice_in_dim(x, length - width, length, axis=dim)
        leading = lax.slice_in_dim(x, 0, width, axis=dim)
        before = lax.ppermute(last, axis, up)
        after = lax.ppermute(leading, axis, down)
        x = jnp.concatenate([before, x, after], axis=dim)
    return x


def entering(part, axis, combine, identity):
    place = lax.axis_index(axis)
    gathered = jax.tree.map(lambda a: lax.all_gather(a, axis), part)
    state = jax.tree.map(lambda a, e: jnp.zeros_like(a) + jnp.asarray(e, a.dtype), part, identity)

    def one(lap, state):
        return combine(
            state, jax.tree.map(lambda a: lax.dynamic_index_in_dim(a, lap, 0, False), gathered)
        )

    return lax.fori_loop(0, place, one, state)


def neighbours(padded):
    center = padded[1:-1, 1:-1]
    z_padded = jnp.pad(center, ((0, 0), (0, 0), (1, 1)))
    return (
        center,
        (
            padded[2:, 1:-1],
            padded[:-2, 1:-1],
            padded[1:-1, 2:],
            padded[1:-1, :-2],
            z_padded[:, :, 2:],
            z_padded[:, :, :-2],
        ),
    )


def face_weights(cond_padded):
    conductivity, beside_all = neighbours(cond_padded)
    return tuple(
        (weight * 0.5 * (conductivity + other) for weight, other in zip(axis_weights, beside_all))
    )


def apply_operator(fields_padded, face_list, coupling):
    solid, solid_around = neighbours(fields_padded[0])
    gas, gas_around = neighbours(fields_padded[1])
    exchange_term = coupling * (solid - gas)
    solid_out = solid_cap * solid + exchange_term
    gas_out = gas_cap * gas - exchange_term + flow_rate * (gas - gas_around[3])
    for face, weight, other_solid, other_gas in zip(
        face_list, axis_weights, solid_around, gas_around
    ):
        solid_out = solid_out + face * (solid - other_solid)
        gas_out = gas_out + gas_conduct * weight * (gas - other_gas)
    return jnp.stack([solid_out, gas_out])


def relax_step(fields, residual, solid_diag, coupling):
    gas_diag = gas_cap + coupling + flow_rate + gas_conduct * 2.0 * 2.25
    determinant = solid_diag * gas_diag - coupling * coupling
    delta_solid = (gas_diag * residual[0] + coupling * residual[1]) / determinant
    delta_gas = (coupling * residual[0] + solid_diag * residual[1]) / determinant
    return fields + relaxation * jnp.stack([delta_solid, delta_gas])


def coarse_sum(array):
    shape = array.shape
    lead = shape[:-3]
    return array.reshape(lead + (shape[-3] // 2, 2, shape[-2] // 2, 2, shape[-1])).sum(
        axis=(-4, -2)
    )


def spread(coarse):
    shape = coarse.shape
    wide = jnp.broadcast_to(
        coarse[:, :, None, :, None, :], (shape[0], shape[1], 2, shape[2], 2, shape[3])
    )
    return wide.reshape((shape[0], shape[1] * 2, shape[2] * 2, shape[3]))


def line_combine(earlier, later):
    return (later[0] * earlier[0], later[0] * earlier[1] + later[1])


def shards(temps, right_side, exchange, coupling):
    conductivity = 1.0 + 4.0 * exchange * temps[0] ** 3
    cond_padded = padded_2(conductivity, (("gx", 0), ("gy", 1)), 1)
    face_list = face_weights(cond_padded)
    solid_diag = solid_cap + coupling + sum(face_list)

    def residual_of(fields):
        padded = padded_2(fields, (("gx", 1), ("gy", 2)), 1)
        return right_side - apply_operator(padded, face_list, coupling)

    def smooth(fields):
        for sweep_index in range(SWEEPS):
            fields = relax_step(fields, residual_of(fields), solid_diag, coupling)
        return fields

    fields = smooth(temps)
    coarse_res = coarse_sum(residual_of(fields))
    coupling_sum = coarse_sum(coupling)
    solid_coarse = 4.0 * solid_cap + coupling_sum + lump_factor * coarse_sum(conductivity)
    gas_coarse = 4.0 * gas_cap + coupling_sum + 2.0 * flow_rate
    denominator = gas_coarse - coupling_sum * coupling_sum / solid_coarse
    slope = 2.0 * flow_rate / denominator
    offset = (coarse_res[1] + coupling_sum * coarse_res[0] / solid_coarse) / denominator
    slope_cum, offset_cum = lax.associative_scan(line_combine, (slope, offset), axis=1)
    block_slope = slope_cum[:, -1, :]
    block_offset = offset_cum[:, -1, :]
    identity = (jnp.ones_like(block_slope), jnp.zeros_like(block_offset))
    prefix_slope, incoming = entering((block_slope, block_offset), "gy", line_combine, identity)
    gas_error = slope_cum * incoming[:, None, :] + offset_cum
    solid_error = (coarse_res[0] + coupling_sum * gas_error) / solid_coarse
    fields = fields + spread(jnp.stack([solid_error, gas_error]))
    return smooth(fields)


def solution(mesh):
    return jax.shard_map(
        shards,
        mesh=mesh,
        in_specs=(
            P(None, "gx", "gy", None),
            P(None, "gx", "gy", None),
            P("gx", "gy", None),
            P("gx", "gy", None),
        ),
        out_specs=P(None, "gx", "gy", None),
        check_vma=False,
    )
```

profile of v0, /device:TPU:247, one launch (start us, length us, event | category | flops | bytes accessed | tf_op | source)
XLA Modules:
  0.0 267.3 jit_solution(918432057127025591)
XLA Ops:
  0.0 1.0 fusion.178
  1.0 5.2 %collective-permute-start = (f32[2,1,12,128]{3,1,2,0:T(1,128)S(1)}, f32[2,1,12,128]{3,1,2,0:T(1,128)S(1)}, u32[]{:S(2)}, u32[]{:S(2)}) collective-permute-start(f32[2,1,12,128]{3,1,2,0:T(1,128)S(1)} %get-tuple-element.105), channel_id=1, source_target_pairs={{0,64},{64,128},{128,192},{192,256},{256,320},{320,384},{384,448},... | collective-permute-start | bytes 36872 | tf_op jit(solution)/shard_map/ppermute | solution.py:25
  6.2 1.9 collective-permute-start.1
  8.2 1.1 fusion.5
  9.2 4.6 %collective-permute-start.5 = (f32[1,12,128]{2,0,1:T(1,128)S(1)}, f32[1,12,128]{2,0,1:T(1,128)S(1)}, u32[]{:S(2)}, u32[]{:S(2)}) collective-permute-start(f32[1,12,128]{2,0,1:T(1,128)S(1)} %get-tuple-element.119), channel_id=1, source_target_pairs={{0,64},{64,128},{128,192},{192,256},{256,320},{320,384},{384,448},... | collective-permute-start | bytes 18440 | tf_op jit(solution)/shard_map/ppermute | solution.py:25
  13.8 1.9 collective-permute-start.4
  15.8 3.6 %collective-permute-start.2 = (f32[2,34,1,128]{3,1,2,0:T(8,128)S(1)}, f32[2,34,1,128]{3,1,2,0:T(8,128)S(1)}, u32[]{:S(2)}, u32[]{:S(2)}) collective-permute-start(f32[2,34,1,128]{3,1,2,0:T(8,128)S(1)} %get-tuple-element.95), channel_id=1, source_target_pairs={{0,1},{1,2},{2,3},{3,4},{4,5},{5,6},{6,7},{7,8},{8,9},{9,10},{10,1... | collective-permute-start | bytes 104456 | tf_op jit(solution)/shard_map/ppermute | solution.py:25
  19.4 1.9 collective-permute-start.3
  21.4 5.8 %collective-permute-start.7 = (f32[34,1,128]{2,0,1:T(8,128)S(1)}, f32[34,1,128]{2,0,1:T(8,128)S(1)}, u32[]{:S(2)}, u32[]{:S(2)}) collective-permute-start(f32[34,1,128]{2,0,1:T(8,128)S(1)} %get-tuple-element.117), channel_id=1, source_target_pairs={{0,1},{1,2},{2,3},{3,4},{4,5},{5,6},{6,7},{7,8},{8,9},{9,10},{10,1... | collective-permute-start | bytes 52232 | tf_op jit(solution)/shard_map/ppermute | solution.py:25
  27.2 1.9 collective-permute-start.6
  29.3 0.9 copy-done
  30.4 4.0 %collective-permute-done.6 = f32[34,1,128]{2,0,1:T(8,128)S(1)} collective-permute-done((f32[34,1,128]{2,0,1:T(8,128)S(1)}, f32[34,1,128]{2,0,1:T(8,128)S(1)}, u32[]{:S(2)}, u32[]{:S(2)}) %collective-permute-start.6) | collective-permute-done | bytes 17440 | tf_op jit(solution)/shard_map/ppermute | solution.py:26
  35.8 4.9 %collective-permute-start.8 = (f32[2,1,12,128]{3,1,2,0:T(1,128)S(1)}, f32[2,1,12,128]{3,1,2,0:T(1,128)S(1)}, u32[]{:S(2)}, u32[]{:S(2)}) collective-permute-start(f32[2,1,12,128]{3,1,2,0:T(1,128)S(1)} %get-tuple-element.103), channel_id=1, source_target_pairs={{0,64},{64,128},{128,192},{192,256},{256,320},{320,384},{384,448},... | collective-permute-start | bytes 36872 | tf_op jit(solution)/shard_map/ppermute | solution.py:25
  40.7 1.9 collective-permute-start.9
  42.6 3.7 %collective-permute-done.9 = f32[2,1,12,128]{3,1,2,0:T(1,128)S(1)} collective-permute-done((f32[2,1,12,128]{3,1,2,0:T(1,128)S(1)}, f32[2,1,12,128]{3,1,2,0:T(1,128)S(1)}, u32[]{:S(2)}, u32[]{:S(2)}) %collective-permute-start.9) | collective-permute-done | bytes 12320 | tf_op jit(solution)/shard_map/ppermute | solution.py:26
  46.4 3.4 %collective-permute-start.10 = (f32[2,34,1,128]{3,1,2,0:T(8,128)S(1)}, f32[2,34,1,128]{3,1,2,0:T(8,128)S(1)}, u32[]{:S(2)}, u32[]{:S(2)}) collective-permute-start(f32[2,34,1,128]{3,1,2,0:T(8,128)S(1)} %get-tuple-element.93), channel_id=1, source_target_pairs={{0,1},{1,2},{2,3},{3,4},{4,5},{5,6},{6,7},{7,8},{8,9},{9,10},{10,1... | collective-permute-start | bytes 104456 | tf_op jit(solution)/shard_map/ppermute | solution.py:25
  49.7 1.9 collective-permute-start.11
  51.7 5.5 %collective-permute-done.11 = f32[2,34,1,128]{3,1,2,0:T(8,128)S(1)} collective-permute-done((f32[2,34,1,128]{3,1,2,0:T(8,128)S(1)}, f32[2,34,1,128]{3,1,2,0:T(8,128)S(1)}, u32[]{:S(2)}, u32[]{:S(2)}) %collective-permute-start.11) | collective-permute-done | bytes 34848 | tf_op jit(solution)/shard_map/ppermute | solution.py:26
  58.2 1.9 collective-permute-start.12
  60.1 3.4 %collective-permute-start.13 = (f32[2,1,12,128]{3,1,2,0:T(1,128)S(1)}, f32[2,1,12,128]{3,1,2,0:T(1,128)S(1)}, u32[]{:S(2)}, u32[]{:S(2)}) collective-permute-start(f32[2,1,12,128]{3,1,2,0:T(1,128)S(1)} %get-tuple-element.102), channel_id=1, source_target_pairs={{64,0},{128,64},{192,128},{256,192},{320,256},{384,320},{448,384},... | collective-permute-start | bytes 36872 | tf_op jit(solution)/shard_map/ppermute | solution.py:26
  63.5 2.3 collective-permute-done.13
  65.8 3.1 %collective-permute-start.14 = (f32[2,34,1,128]{3,1,2,0:T(8,128)S(1)}, f32[2,34,1,128]{3,1,2,0:T(8,128)S(1)}, u32[]{:S(2)}, u32[]{:S(2)}) collective-permute-start(f32[2,34,1,128]{3,1,2,0:T(8,128)S(1)} %get-tuple-element.91), channel_id=1, source_target_pairs={{0,1},{1,2},{2,3},{3,4},{4,5},{5,6},{6,7},{7,8},{8,9},{9,10},{10,1... | collective-permute-start | bytes 104456 | tf_op jit(solution)/shard_map/ppermute | solution.py:25
  68.8 1.9 collective-permute-start.15
  71.1 5.2 %collective-permute-done.15 = f32[2,34,1,128]{3,1,2,0:T(8,128)S(1)} collective-permute-done((f32[2,34,1,128]{3,1,2,0:T(8,128)S(1)}, f32[2,34,1,128]{3,1,2,0:T(8,128)S(1)}, u32[]{:S(2)}, u32[]{:S(2)}) %collective-permute-start.15) | collective-permute-done | bytes 34848 | tf_op jit(solution)/shard_map/ppermute | solution.py:26
  77.7 51.4 %all-gather.1 = f32[1024,1,128]{2,0,1:T(8,128)S(1)} all-gather(f32[16,1,128]{2,0,1:T(8,128)S(1)} %slice_add_fusion.1), channel_id=3, replica_groups=mesh['gx'=12,'gy'=64] {'gy'}, dimensions={0}, use_global_device_ids=true | all-gather | bytes 532480 | tf_op jit(solution)/shard_map/all_gather | solution.py:33
  129.1 54.3 %all-gather = f32[1024,1,128]{2,0,1:T(8,128)} all-gather(f32[16,1,128]{2,0,1:T(8,128)S(1)} %slice_add_fusion.4), channel_id=2, replica_groups=mesh['gx'=12,'gy'=64] {'gy'}, dimensions={0}, use_global_device_ids=true | all-gather | bytes 532480 | tf_op jit(solution)/shard_map/all_gather | solution.py:33
  183.4 38.6 %while.12 = (s32[]{:T(128)}, f32[16,128]{1,0:T(8,128)S(1)}, s32[]{:T(128)}, f32[64,16,128]{2,1,0:T(8,128)}, f32[64,16,128]{2,1,0:T(8,128)S(1)}, /*index=5*/s32[]{:T(128)}, s32[]{:T(128)}, s32[]{:T(128)}) while((s32[]{:T(128)}, f32[16,128]{1,0:T(8,128)S(1)}, s32[]{:T(128)}, f32[64,16,128]{2,1,0:T(8,128)}, f32[64,16,128]{2,1,0:T(8,128)S(1)}, ...), condition=%wide.region_4.5_spmd, body=%wide.region_3.4_spmd.sunk | while | flops 4101 | bytes 32899 | solution.py:41
  183.4 0.7 bitcast_add_fusion.2
  187.6 0.7 bitcast_add_fusion.2
  188.3 0.7 bitcast_add_fusion.2
  189.0 0.7 bitcast_add_fusion.2
  189.8 0.7 bitcast_add_fusion.2
  190.5 0.7 bitcast_add_fusion.2
  191.2 0.7 bitcast_add_fusion.2
  191.9 0.7 bitcast_add_fusion.2
  192.6 0.7 bitcast_add_fusion.2
  193.3 0.7 bitcast_add_fusion.2
  194.0 0.7 bitcast_add_fusion.2
  194.7 0.7 bitcast_add_fusion.2
  195.4 0.7 bitcast_add_fusion.2
  201.0 0.7 bitcast_add_fusion.2
  201.7 0.7 bitcast_add_fusion.2
  202.4 0.7 bitcast_add_fusion.2
  203.1 0.7 bitcast_add_fusion.2
  203.8 0.7 bitcast_add_fusion.2
  204.5 0.7 bitcast_add_fusion.2
  205.2 0.7 bitcast_add_fusion.2
  205.9 0.7 bitcast_add_fusion.2
  206.6 0.7 bitcast_add_fusion.2
  207.3 0.7 bitcast_add_fusion.2
  208.0 0.7 bitcast_add_fusion.2
  222.5 3.5 %collective-permute-start.16 = (f32[2,1,12,128]{3,1,2,0:T(1,128)S(1)}, f32[2,1,12,128]{3,1,2,0:T(1,128)S(1)}, u32[]{:S(2)}, u32[]{:S(2)}) collective-permute-start(f32[2,1,12,128]{3,1,2,0:T(1,128)S(1)} %get-tuple-element.99), channel_id=1, source_target_pairs={{0,64},{64,128},{128,192},{192,256},{256,320},{320,384},{384,448},... | collective-permute-start | bytes 36872 | tf_op jit(solution)/shard_map/ppermute | solution.py:25
  225.9 1.9 collective-permute-start.17
  227.9 4.2 %collective-permute-done.17 = f32[2,1,12,128]{3,1,2,0:T(1,128)S(1)} collective-permute-done((f32[2,1,12,128]{3,1,2,0:T(1,128)S(1)}, f32[2,1,12,128]{3,1,2,0:T(1,128)S(1)}, u32[]{:S(2)}, u32[]{:S(2)}) %collective-permute-start.17) | collective-permute-done | bytes 12320 | tf_op jit(solution)/shard_map/ppermute | solution.py:26
  232.1 4.9 %collective-permute-start.18 = (f32[2,34,1,128]{3,1,2,0:T(8,128)S(1)}, f32[2,34,1,128]{3,1,2,0:T(8,128)S(1)}, u32[]{:S(2)}, u32[]{:S(2)}) collective-permute-start(f32[2,34,1,128]{3,1,2,0:T(8,128)S(1)} %get-tuple-element.89), channel_id=1, source_target_pairs={{0,1},{1,2},{2,3},{3,4},{4,5},{5,6},{6,7},{7,8},{8,9},{9,10},{10,1... | collective-permute-start | bytes 104456 | tf_op jit(solution)/shard_map/ppermute | solution.py:25
  237.1 1.9 collective-permute-start.19
  239.0 5.5 %collective-permute-done.19 = f32[2,34,1,128]{3,1,2,0:T(8,128)S(1)} collective-permute-done((f32[2,34,1,128]{3,1,2,0:T(8,128)S(1)}, f32[2,34,1,128]{3,1,2,0:T(8,128)S(1)}, u32[]{:S(2)}, u32[]{:S(2)}) %collective-permute-start.19) | collective-permute-done | bytes 34848 | tf_op jit(solution)/shard_map/ppermute | solution.py:26
  245.5 3.6 %collective-permute-start.20 = (f32[2,1,12,128]{3,1,2,0:T(1,128)S(1)}, f32[2,1,12,128]{3,1,2,0:T(1,128)S(1)}, u32[]{:S(2)}, u32[]{:S(2)}) collective-permute-start(f32[2,1,12,128]{3,1,2,0:T(1,128)S(1)} %get-tuple-element.97), channel_id=1, source_target_pairs={{0,64},{64,128},{128,192},{192,256},{256,320},{320,384},{384,448},... | collective-permute-start | bytes 36872 | tf_op jit(solution)/shard_map/ppermute | solution.py:25
  249.1 1.9 collective-permute-start.21
  251.1 3.7 %collective-permute-done.21 = f32[2,1,12,128]{3,1,2,0:T(1,128)S(1)} collective-permute-done((f32[2,1,12,128]{3,1,2,0:T(1,128)S(1)}, f32[2,1,12,128]{3,1,2,0:T(1,128)S(1)}, u32[]{:S(2)}, u32[]{:S(2)}) %collective-permute-start.21) | collective-permute-done | bytes 12320 | tf_op jit(solution)/shard_map/ppermute | solution.py:26
  254.8 3.3 %collective-permute-start.22 = (f32[2,34,1,128]{3,1,2,0:T(8,128)S(1)}, f32[2,34,1,128]{3,1,2,0:T(8,128)S(1)}, u32[]{:S(2)}, u32[]{:S(2)}) collective-permute-start(f32[2,34,1,128]{3,1,2,0:T(8,128)S(1)} %get-tuple-element.87), channel_id=1, source_target_pairs={{0,1},{1,2},{2,3},{3,4},{4,5},{5,6},{6,7},{7,8},{8,9},{9,10},{10,1... | collective-permute-start | bytes 104456 | tf_op jit(solution)/shard_map/ppermute | solution.py:25
  258.1 1.9 collective-permute-start.23
  260.1 5.5 %collective-permute-done.23 = f32[2,34,1,128]{3,1,2,0:T(8,128)S(1)} collective-permute-done((f32[2,34,1,128]{3,1,2,0:T(8,128)S(1)}, f32[2,34,1,128]{3,1,2,0:T(8,128)S(1)}, u32[]{:S(2)}, u32[]{:S(2)}) %collective-permute-start.23) | collective-permute-done | bytes 34848 | tf_op jit(solution)/shard_map/ppermute | solution.py:26
  266.4 0.9 fusion.3
  (127 shorter events, 28.4 us)
Async XLA Ops:
  0.0 15.8 %copy-start.1 = (f32[2,32,12,128]{3,1,2,0:T(8,128)S(1)}, f32[2,32,12,128]{3,1,2,0:T(8,128)}, u32[]{:S(2)}) copy-start(f32[2,32,12,128]{3,1,2,0:T(8,128)} %param.6) | copy-start | bytes 1179652
  1.0 14.7 %collective-permute-start = (f32[2,1,12,128]{3,1,2,0:T(1,128)S(1)}, f32[2,1,12,128]{3,1,2,0:T(1,128)S(1)}, u32[]{:S(2)}, u32[]{:S(2)}) collective-permute-start(f32[2,1,12,128]{3,1,2,0:T(1,128)S(1)} %get-tuple-element.105), channel_id=1, source_target_pairs={{0,64},{64,128},{128,192},{192,256},{256,320},{320,384},{384,448},... | collective-permute-start | bytes 36872 | tf_op jit(solution)/shard_map/ppermute | solution.py:25
  6.2 9.5 %collective-permute-start.1 = (f32[2,1,12,128]{3,1,2,0:T(1,128)S(1)}, f32[2,1,12,128]{3,1,2,0:T(1,128)S(1)}, u32[]{:S(2)}, u32[]{:S(2)}) collective-permute-start(f32[2,1,12,128]{3,1,2,0:T(1,128)S(1)} %get-tuple-element.106), channel_id=1, source_target_pairs={{64,0},{128,64},{192,128},{256,192},{320,256},{384,320},{448,384},... | collective-permute-start | bytes 36872 | tf_op jit(solution)/shard_map/ppermute | solution.py:26
  9.2 12.1 %collective-permute-start.5 = (f32[1,12,128]{2,0,1:T(1,128)S(1)}, f32[1,12,128]{2,0,1:T(1,128)S(1)}, u32[]{:S(2)}, u32[]{:S(2)}) collective-permute-start(f32[1,12,128]{2,0,1:T(1,128)S(1)} %get-tuple-element.119), channel_id=1, source_target_pairs={{0,64},{64,128},{128,192},{192,256},{256,320},{320,384},{384,448},... | collective-permute-start | bytes 18440 | tf_op jit(solution)/shard_map/ppermute | solution.py:25
  13.8 7.6 %collective-permute-start.4 = (f32[1,12,128]{2,0,1:T(1,128)S(1)}, f32[1,12,128]{2,0,1:T(1,128)S(1)}, u32[]{:S(2)}, u32[]{:S(2)}) collective-permute-start(f32[1,12,128]{2,0,1:T(1,128)S(1)} %get-tuple-element.120), channel_id=1, source_target_pairs={{64,0},{128,64},{192,128},{256,192},{320,256},{384,320},{448,384},... | collective-permute-start | bytes 18440 | tf_op jit(solution)/shard_map/ppermute | solution.py:26
  15.8 13.3 %collective-permute-start.2 = (f32[2,34,1,128]{3,1,2,0:T(8,128)S(1)}, f32[2,34,1,128]{3,1,2,0:T(8,128)S(1)}, u32[]{:S(2)}, u32[]{:S(2)}) collective-permute-start(f32[2,34,1,128]{3,1,2,0:T(8,128)S(1)} %get-tuple-element.95), channel_id=1, source_target_pairs={{0,1},{1,2},{2,3},{3,4},{4,5},{5,6},{6,7},{7,8},{8,9},{9,10},{10,1... | collective-permute-start | bytes 104456 | tf_op jit(solution)/shard_map/ppermute | solution.py:25
  19.4 9.7 %collective-permute-start.3 = (f32[2,34,1,128]{3,1,2,0:T(8,128)S(1)}, f32[2,34,1,128]{3,1,2,0:T(8,128)S(1)}, u32[]{:S(2)}, u32[]{:S(2)}) collective-permute-start(f32[2,34,1,128]{3,1,2,0:T(8,128)S(1)} %get-tuple-element.96), channel_id=1, source_target_pairs={{1,0},{2,1},{3,2},{4,3},{5,4},{6,5},{7,6},{8,7},{9,8},{10,9},{11,1... | collective-permute-start | bytes 104456 | tf_op jit(solution)/shard_map/ppermute | solution.py:26
  21.4 9.0 %collective-permute-start.7 = (f32[34,1,128]{2,0,1:T(8,128)S(1)}, f32[34,1,128]{2,0,1:T(8,128)S(1)}, u32[]{:S(2)}, u32[]{:S(2)}) collective-permute-start(f32[34,1,128]{2,0,1:T(8,128)S(1)} %get-tuple-element.117), channel_id=1, source_target_pairs={{0,1},{1,2},{2,3},{3,4},{4,5},{5,6},{6,7},{7,8},{8,9},{9,10},{10,1... | collective-permute-start | bytes 52232 | tf_op jit(solution)/shard_map/ppermute | solution.py:25
  27.2 7.2 %collective-permute-start.6 = (f32[34,1,128]{2,0,1:T(8,128)S(1)}, f32[34,1,128]{2,0,1:T(8,128)S(1)}, u32[]{:S(2)}, u32[]{:S(2)}) collective-permute-start(f32[34,1,128]{2,0,1:T(8,128)S(1)} %get-tuple-element.118), channel_id=1, source_target_pairs={{1,0},{2,1},{3,2},{4,3},{5,4},{6,5},{7,6},{8,7},{9,8},{10,9},{11,1... | collective-permute-start | bytes 52232 | tf_op jit(solution)/shard_map/ppermute | solution.py:26
  29.2 0.9 copy-start
  34.4 1.0 copy-start.2
  35.8 6.8 %collective-permute-start.8 = (f32[2,1,12,128]{3,1,2,0:T(1,128)S(1)}, f32[2,1,12,128]{3,1,2,0:T(1,128)S(1)}, u32[]{:S(2)}, u32[]{:S(2)}) collective-permute-start(f32[2,1,12,128]{3,1,2,0:T(1,128)S(1)} %get-tuple-element.103), channel_id=1, source_target_pairs={{0,64},{64,128},{128,192},{192,256},{256,320},{320,384},{384,448},... | collective-permute-start | bytes 36872 | tf_op jit(solution)/shard_map/ppermute | solution.py:25
  40.7 5.7 %collective-permute-start.9 = (f32[2,1,12,128]{3,1,2,0:T(1,128)S(1)}, f32[2,1,12,128]{3,1,2,0:T(1,128)S(1)}, u32[]{:S(2)}, u32[]{:S(2)}) collective-permute-start(f32[2,1,12,128]{3,1,2,0:T(1,128)S(1)} %get-tuple-element.104), channel_id=1, source_target_pairs={{64,0},{128,64},{192,128},{256,192},{320,256},{384,320},{448,384},... | collective-permute-start | bytes 36872 | tf_op jit(solution)/shard_map/ppermute | solution.py:26
  46.4 5.3 %collective-permute-start.10 = (f32[2,34,1,128]{3,1,2,0:T(8,128)S(1)}, f32[2,34,1,128]{3,1,2,0:T(8,128)S(1)}, u32[]{:S(2)}, u32[]{:S(2)}) collective-permute-start(f32[2,34,1,128]{3,1,2,0:T(8,128)S(1)} %get-tuple-element.93), channel_id=1, source_target_pairs={{0,1},{1,2},{2,3},{3,4},{4,5},{5,6},{6,7},{7,8},{8,9},{9,10},{10,1... | collective-permute-start | bytes 104456 | tf_op jit(solution)/shard_map/ppermute | solution.py:25
  49.7 7.4 %collective-permute-start.11 = (f32[2,34,1,128]{3,1,2,0:T(8,128)S(1)}, f32[2,34,1,128]{3,1,2,0:T(8,128)S(1)}, u32[]{:S(2)}, u32[]{:S(2)}) collective-permute-start(f32[2,34,1,128]{3,1,2,0:T(8,128)S(1)} %get-tuple-element.94), channel_id=1, source_target_pairs={{1,0},{2,1},{3,2},{4,3},{5,4},{6,5},{7,6},{8,7},{9,8},{10,9},{11,1... | collective-permute-start | bytes 104456 | tf_op jit(solution)/shard_map/ppermute | solution.py:26
  58.2 5.3 %collective-permute-start.12 = (f32[2,1,12,128]{3,1,2,0:T(1,128)S(1)}, f32[2,1,12,128]{3,1,2,0:T(1,128)S(1)}, u32[]{:S(2)}, u32[]{:S(2)}) collective-permute-start(f32[2,1,12,128]{3,1,2,0:T(1,128)S(1)} %get-tuple-element.101), channel_id=1, source_target_pairs={{0,64},{64,128},{128,192},{192,256},{256,320},{320,384},{384,448},... | collective-permute-start | bytes 36872 | tf_op jit(solution)/shard_map/ppermute | solution.py:25
  60.1 5.7 %collective-permute-start.13 = (f32[2,1,12,128]{3,1,2,0:T(1,128)S(1)}, f32[2,1,12,128]{3,1,2,0:T(1,128)S(1)}, u32[]{:S(2)}, u32[]{:S(2)}) collective-permute-start(f32[2,1,12,128]{3,1,2,0:T(1,128)S(1)} %get-tuple-element.102), channel_id=1, source_target_pairs={{64,0},{128,64},{192,128},{256,192},{320,256},{384,320},{448,384},... | collective-permute-start | bytes 36872 | tf_op jit(solution)/shard_map/ppermute | solution.py:26
  65.8 5.3 %collective-permute-start.14 = (f32[2,34,1,128]{3,1,2,0:T(8,128)S(1)}, f32[2,34,1,128]{3,1,2,0:T(8,128)S(1)}, u32[]{:S(2)}, u32[]{:S(2)}) collective-permute-start(f32[2,34,1,128]{3,1,2,0:T(8,128)S(1)} %get-tuple-element.91), channel_id=1, source_target_pairs={{0,1},{1,2},{2,3},{3,4},{4,5},{5,6},{6,7},{7,8},{8,9},{9,10},{10,1... | collective-permute-start | bytes 104456 | tf_op jit(solution)/shard_map/ppermute | solution.py:25
  68.8 7.4 %collective-permute-start.15 = (f32[2,34,1,128]{3,1,2,0:T(8,128)S(1)}, f32[2,34,1,128]{3,1,2,0:T(8,128)S(1)}, u32[]{:S(2)}, u32[]{:S(2)}) collective-permute-start(f32[2,34,1,128]{3,1,2,0:T(8,128)S(1)} %get-tuple-element.92), channel_id=1, source_target_pairs={{1,0},{2,1},{3,2},{4,3},{5,4},{6,5},{7,6},{8,7},{9,8},{10,9},{11,1... | collective-permute-start | bytes 104456 | tf_op jit(solution)/shard_map/ppermute | solution.py:26
  222.5 5.4 %collective-permute-start.16 = (f32[2,1,12,128]{3,1,2,0:T(1,128)S(1)}, f32[2,1,12,128]{3,1,2,0:T(1,128)S(1)}, u32[]{:S(2)}, u32[]{:S(2)}) collective-permute-start(f32[2,1,12,128]{3,1,2,0:T(1,128)S(1)} %get-tuple-element.99), channel_id=1, source_target_pairs={{0,64},{64,128},{128,192},{192,256},{256,320},{320,384},{384,448},... | collective-permute-start | bytes 36872 | tf_op jit(solution)/shard_map/ppermute | solution.py:25
  225.9 6.2 %collective-permute-start.17 = (f32[2,1,12,128]{3,1,2,0:T(1,128)S(1)}, f32[2,1,12,128]{3,1,2,0:T(1,128)S(1)}, u32[]{:S(2)}, u32[]{:S(2)}) collective-permute-start(f32[2,1,12,128]{3,1,2,0:T(1,128)S(1)} %get-tuple-element.100), channel_id=1, source_target_pairs={{64,0},{128,64},{192,128},{256,192},{320,256},{384,320},{448,384},... | collective-permute-start | bytes 36872 | tf_op jit(solution)/shard_map/ppermute | solution.py:26
  232.1 6.9 %collective-permute-start.18 = (f32[2,34,1,128]{3,1,2,0:T(8,128)S(1)}, f32[2,34,1,128]{3,1,2,0:T(8,128)S(1)}, u32[]{:S(2)}, u32[]{:S(2)}) collective-permute-start(f32[2,34,1,128]{3,1,2,0:T(8,128)S(1)} %get-tuple-element.89), channel_id=1, source_target_pairs={{0,1},{1,2},{2,3},{3,4},{4,5},{5,6},{6,7},{7,8},{8,9},{9,10},{10,1... | collective-permute-start | bytes 104456 | tf_op jit(solution)/shard_map/ppermute | solution.py:25
  237.1 7.4 %collective-permute-start.19 = (f32[2,34,1,128]{3,1,2,0:T(8,128)S(1)}, f32[2,34,1,128]{3,1,2,0:T(8,128)S(1)}, u32[]{:S(2)}, u32[]{:S(2)}) collective-permute-start(f32[2,34,1,128]{3,1,2,0:T(8,128)S(1)} %get-tuple-element.90), channel_id=1, source_target_pairs={{1,0},{2,1},{3,2},{4,3},{5,4},{6,5},{7,6},{8,7},{9,8},{10,9},{11,1... | collective-permute-start | bytes 104456 | tf_op jit(solution)/shard_map/ppermute | solution.py:26
  245.5 5.6 %collective-permute-start.20 = (f32[2,1,12,128]{3,1,2,0:T(1,128)S(1)}, f32[2,1,12,128]{3,1,2,0:T(1,128)S(1)}, u32[]{:S(2)}, u32[]{:S(2)}) collective-permute-start(f32[2,1,12,128]{3,1,2,0:T(1,128)S(1)} %get-tuple-element.97), channel_id=1, source_target_pairs={{0,64},{64,128},{128,192},{192,256},{256,320},{320,384},{384,448},... | collective-permute-start | bytes 36872 | tf_op jit(solution)/shard_map/ppermute | solution.py:25
  249.1 5.7 %collective-permute-start.21 = (f32[2,1,12,128]{3,1,2,0:T(1,128)S(1)}, f32[2,1,12,128]{3,1,2,0:T(1,128)S(1)}, u32[]{:S(2)}, u32[]{:S(2)}) collective-permute-start(f32[2,1,12,128]{3,1,2,0:T(1,128)S(1)} %get-tuple-element.98), channel_id=1, source_target_pairs={{64,0},{128,64},{192,128},{256,192},{320,256},{384,320},{448,384},... | collective-permute-start | bytes 36872 | tf_op jit(solution)/shard_map/ppermute | solution.py:26
  254.8 5.3 %collective-permute-start.22 = (f32[2,34,1,128]{3,1,2,0:T(8,128)S(1)}, f32[2,34,1,128]{3,1,2,0:T(8,128)S(1)}, u32[]{:S(2)}, u32[]{:S(2)}) collective-permute-start(f32[2,34,1,128]{3,1,2,0:T(8,128)S(1)} %get-tuple-element.87), channel_id=1, source_target_pairs={{0,1},{1,2},{2,3},{3,4},{4,5},{5,6},{6,7},{7,8},{8,9},{9,10},{10,1... | collective-permute-start | bytes 104456 | tf_op jit(solution)/shard_map/ppermute | solution.py:25
  258.1 7.4 %collective-permute-start.23 = (f32[2,34,1,128]{3,1,2,0:T(8,128)S(1)}, f32[2,34,1,128]{3,1,2,0:T(8,128)S(1)}, u32[]{:S(2)}, u32[]{:S(2)}) collective-permute-start(f32[2,34,1,128]{3,1,2,0:T(8,128)S(1)} %get-tuple-element.88), channel_id=1, source_target_pairs={{1,0},{2,1},{3,2},{4,3},{5,4},{6,5},{7,6},{8,7},{9,8},{10,9},{11,1... | collective-permute-start | bytes 104456 | tf_op jit(solution)/shard_map/ppermute | solution.py:26
where the time goes:
time: 272 us; the launch traced here: 267 us
  blocking collectives  106 us (39%)
  starting transfers between devices  72.2 us (27%)
  other arithmetic  45.8 us (17%)
  waiting for transfers between devices  39.6 us (15%)
  local copies, waits for them, and re-layouts  3.24 us (1%)
    all_gather x2, blocking collectives, entering(): gathered = jax.tree.map(lambda a: lax.all_gather(a, axis), part)  106 us
    ppermute x12, starting transfers between devices, padded_2(): before = lax.ppermute(last, axis, up)  47.7 us
    ppermute x12, waiting for transfers between devices, padded_2(): after = lax.ppermute(leading, axis, down)  39.6 us
    add x55, other arithmetic, line_combine(): return (later[0] * earlier[0], later[0] * earlier[1] + later[1])  38.6 us
    ppermute x12, starting transfers between devices, padded_2(): after = lax.ppermute(leading, axis, down)  24.5 us
  transfers between devices with their start and end apart: 24, of which 9 were waited for; matrix products, arithmetic and copies ran while one was open for 1% of the time, Pallas kernels for 0%

commit v1 on v0

v1 whole, which is shorter than its diff:
```python
import functools

import jax
import jax.numpy as jnp
from jax import lax
from jax.experimental import pallas as pl
from jax.experimental.pallas import tpu as pltpu
from jax.sharding import PartitionSpec as P

MESH = pl.DeviceIdType.MESH
PITCH = 16
CHUNK = 64

solid_cap = 0.5
gas_cap = 0.02
flow_rate = 40.0
gas_conduct = 0.05
relaxation = 0.8
lump_factor = 0.25
STAGES = 5


def kernel(dims, temps, right, exch, coup, out, *scratch):
    nx, ny, nz, n_gx, n_gy, group = dims
    rows = nx * PITCH
    cx, cy = nx // 2, ny // 2
    n_group = n_gy // group
    (t_in, b_in, e_in, c_in, o_v, f0, f1, f2, f3, f4, b_f, c_f, fx, fy, fz, diag, pp, qq, rr, res,
     ys, yr, slopes, csum, isol, iden, cres, offs, s_blk, o_blk, s_rec, o_rec, s_row, o_row, s_rrec, o_rrec, s_pre,
     in_sem, h_send, h_recv, g_send, g_recv) = scratch
    ix, iy = lax.axis_index("gx"), lax.axis_index("gy")
    place, row = lax.rem(iy, group), lax.div(iy, group)

    loads = [
        pltpu.make_async_copy(src, dst, in_sem.at[i])
        for i, (src, dst) in enumerate(((temps, t_in), (exch, e_in), (coup, c_in), (right, b_in)))
    ]
    for load in loads:
        load.start()

    barrier = pltpu.get_barrier_semaphore()

    def greet(gx, gy):
        pl.semaphore_signal(barrier, inc=1, device_id=(gx, gy), device_id_type=MESH)

    for d in range(1, group):
        greet(ix, row * group + lax.rem(place + d, group))
    for d in range(1, n_group):
        greet(ix, lax.rem(row + d, n_group) * group + place)
    up_y, down_y, up_x, down_x = iy < n_gy - 1, iy > 0, ix < n_gx - 1, ix > 0
    pl.when(up_y)(lambda: greet(ix, iy + 1))
    pl.when(down_y)(lambda: greet(ix, iy - 1))
    pl.when(up_x)(lambda: greet(ix + 1, iy))
    pl.when(down_x)(lambda: greet(ix - 1, iy))

    fields = (f0, f1, f2, f3, f4)
    slab_zero = jnp.zeros((PITCH, nz), jnp.float32)
    plane_zero = jnp.zeros((nx, nz), jnp.float32)

    def clear_slabs(at):
        for f in fields:
            for n in range(f.shape[0]):
                f[n, at:at + PITCH, :] = slab_zero

    def clear_planes(side):
        for st in range(STAGES):
            for n in range(3 if st == 0 else 2):
                yr[st, side, n] = plane_zero

    pl.when(jnp.logical_not(down_x))(lambda: clear_slabs(0))
    pl.when(jnp.logical_not(up_x))(lambda: clear_slabs(rows + PITCH))
    pl.when(jnp.logical_not(down_y))(lambda: clear_planes(0))
    pl.when(jnp.logical_not(up_y))(lambda: clear_planes(1))
    for d in range(1, n_group):

        @pl.when(row < d)
        def _():
            s_rrec[d - 1] = jnp.ones((cx, nz), jnp.float32)
            o_rrec[d - 1] = jnp.zeros((cx, nz), jnp.float32)

    def halo_copies(st):
        f = fields[st]
        nf = f.shape[0]
        parts = (
            (up_y, down_y, ys.at[st, 1, :nf], yr.at[st, 0, :nf], (ix, iy + 1)),
            (down_y, up_y, ys.at[st, 0, :nf], yr.at[st, 1, :nf], (ix, iy - 1)),
            (up_x, down_x, f.at[:, rows:rows + PITCH], f.at[:, 0:PITCH], (ix + 1, iy)),
            (down_x, up_x, f.at[:, PITCH:2 * PITCH], f.at[:, rows + PITCH:rows + 2 * PITCH], (ix - 1, iy)),
        )
        return [
            (sends, receives, pltpu.make_async_remote_copy(
                src_ref=src, dst_ref=dst, send_sem=h_send.at[st, i], recv_sem=h_recv.at[st, i],
                device_id=to, device_id_type=MESH))
            for i, (sends, receives, src, dst, to) in enumerate(parts)
        ]

    def send_halo(st):
        f = fields[st]
        for n in range(f.shape[0]):
            ys[st, 0, n] = f[n, pl.ds(PITCH, nx, stride=PITCH), :]
            ys[st, 1, n] = f[n, pl.ds(PITCH + ny - 1, nx, stride=PITCH), :]
        for sends, _, copy in halo_copies(st):
            pl.when(sends)(copy.start)

    def take_halo(st):
        f = fields[st]
        for sends, receives, copy in halo_copies(st):
            pl.when(sends)(copy.wait_send)
            pl.when(receives)(copy.wait_recv)
        for n in range(f.shape[0]):
            f[n, pl.ds(PITCH - 1, nx, stride=PITCH), :] = yr[st, 0, n]
            f[n, pl.ds(PITCH + ny, nx, stride=PITCH), :] = yr[st, 1, n]

    def group_copies(kind, block, received):
        return [
            pltpu.make_async_remote_copy(
                src_ref=block, dst_ref=received.at[d - 1],
                send_sem=g_send.at[kind, d - 1], recv_sem=g_recv.at[kind, d - 1],
                device_id=(ix, row * group + lax.rem(place + d, group)), device_id_type=MESH)
            for d in range(1, group)
        ]

    def row_copies(kind, block, received):
        return [
            (row + d < n_group, row >= d, pltpu.make_async_remote_copy(
                src_ref=block, dst_ref=received.at[d - 1],
                send_sem=g_send.at[kind, d - 1], recv_sem=g_recv.at[kind, d - 1],
                device_id=(ix, (row + d) * group + place), device_id_type=MESH))
            for d in range(1, n_group)
        ]

    loads[0].wait()
    loads[1].wait()

    def spread_in(x, _):
        at = pl.multiple_of((x + 1) * PITCH, PITCH)
        s = t_in[0, x]
        f0[0, pl.ds(at, ny), :] = s
        f0[1, pl.ds(at, ny), :] = t_in[1, x]
        f0[2, pl.ds(at, ny), :] = 1.0 + 4.0 * e_in[x] * (s * s * s)
        return 0

    lax.fori_loop(0, nx, spread_in, 0, unroll=4)
    n_halo = sum(v.astype(jnp.int32) for v in (up_y, down_y, up_x, down_x))
    pl.semaphore_wait(barrier, (group - 1) + (n_group - 1) + n_halo)
    send_halo(0)

    loads[2].wait()
    loads[3].wait()

    def spread_more(x, _):
        at = pl.multiple_of(x * PITCH, PITCH)
        c_f[pl.ds(at, ny), :] = c_in[x]
        b_f[0, pl.ds(at, ny), :] = b_in[0, x]
        b_f[1, pl.ds(at, ny), :] = b_in[1, x]
        return 0

    lax.fori_loop(0, nx, spread_more, 0, unroll=4)

    def block_sum(load, j):
        total = None
        for a in (0, PITCH):
            for b in (0, 1):
                part = load(pl.ds(2 * j + a + b, cx, stride=2 * PITCH))
                total = part if total is None else total + part
        return total

    s_all = None
    for j in range(cy):
        cs = block_sum(lambda at: c_f[at, :], j)
        cond = block_sum(lambda at: f0[2, pl.ds(at.start + PITCH, at.size, stride=at.stride), :], j)
        inv_solid = 1.0 / (4.0 * solid_cap + cs + lump_factor * cond)
        inv_denom = 1.0 / (4.0 * gas_cap + cs + 2.0 * flow_rate - cs * cs * inv_solid)
        slope = 2.0 * flow_rate * inv_denom
        csum[j], isol[j], iden[j], slopes[j] = cs, inv_solid, inv_denom, slope
        s_all = slope if s_all is None else s_all * slope
    s_blk[...] = s_all
    for copy in group_copies(0, s_blk, s_rec):
        copy.start()

    take_halo(0)

    lane = lax.broadcasted_iota(jnp.int32, (CHUNK, nz), 1)
    not_last, not_first = lane < nz - 1, lane > 0
    gas_zp = jnp.where(not_last, gas_conduct * 0.25, 0.0)
    gas_zm = jnp.where(not_first, gas_conduct * 0.25, 0.0)
    fx[0:PITCH] = 0.5 * (f0[2, 0:PITCH, :] + f0[2, PITCH:2 * PITCH, :])
    fy[0:8] = 0.5 * (f0[2, PITCH - 8:PITCH, :] + f0[2, PITCH - 7:PITCH + 1, :])

    def chunks(body):
        def step(i, _):
            body(pl.multiple_of(i * CHUNK, CHUNK))
            return 0

        lax.fori_loop(0, rows // CHUNK, step, 0)

    def set_up(at):
        c = f0[2, pl.ds(at + PITCH, CHUNK), :]
        xp = 0.5 * (c + f0[2, pl.ds(at + 2 * PITCH, CHUNK), :])
        xm = 0.5 * (c + f0[2, pl.ds(at, CHUNK), :])
        yp = 0.5 * (c + f0[2, pl.ds(at + PITCH + 1, CHUNK), :])
        ym = 0.5 * (c + f0[2, pl.ds(at + PITCH - 1, CHUNK), :])
        zp = 0.125 * (c + jnp.where(not_last, pltpu.roll(c, nz - 1, 1), 0.0))
        zm = 0.125 * (c + jnp.where(not_first, pltpu.roll(c, 1, 1), 0.0))
        fx[pl.ds(at + PITCH, CHUNK), :] = xp
        fy[pl.ds(at + 8, CHUNK), :] = yp
        fz[pl.ds(at, CHUNK), :] = jnp.where(not_last, zp, 0.0)
        k = c_f[pl.ds(at, CHUNK), :]
        sd = solid_cap + k + (((xp + xm) + (yp + ym)) + (zp + zm))
        gd = (gas_cap + flow_rate + gas_conduct * 2.0 * 2.25) + k
        w = relaxation / (sd * gd - k * k)
        diag[pl.ds(at, CHUNK), :] = sd
        pp[pl.ds(at, CHUNK), :] = gd * w
        qq[pl.ds(at, CHUNK), :] = k * w
        rr[pl.ds(at, CHUNK), :] = sd * w

    chunks(set_up)

    def beside(f, at):
        s = f[0, pl.ds(at + PITCH, CHUNK), :]
        g = f[1, pl.ds(at + PITCH, CHUNK), :]
        z = fz[pl.ds(at, CHUNK), :]
        hs = b_f[0, pl.ds(at, CHUNK), :]
        hs += fx[pl.ds(at + PITCH, CHUNK), :] * f[0, pl.ds(at + 2 * PITCH, CHUNK), :]
        hs += fx[pl.ds(at, CHUNK), :] * f[0, pl.ds(at, CHUNK), :]
        hs += fy[pl.ds(at + 8, CHUNK), :] * f[0, pl.ds(at + PITCH + 1, CHUNK), :]
        hs += fy[pl.ds(at + 7, CHUNK), :] * f[0, pl.ds(at + PITCH - 1, CHUNK), :]
        hs += z * pltpu.roll(s, nz - 1, 1) + pltpu.roll(z * s, 1, 1)
        hg = b_f[1, pl.ds(at, CHUNK), :]
        hg += (flow_rate + gas_conduct) * f[1, pl.ds(at + PITCH - 1, CHUNK), :]
        hg += gas_conduct * (
            f[1, pl.ds(at + PITCH + 1, CHUNK), :]
            + (f[1, pl.ds(at, CHUNK), :] + f[1, pl.ds(at + 2 * PITCH, CHUNK), :]))
        hg += gas_zp * pltpu.roll(g, nz - 1, 1) + gas_zm * pltpu.roll(g, 1, 1)
        return s, g, hs, hg

    def relaxed(f, at):
        s, g, hs, hg = beside(f, at)
        p, q, r = (ref[pl.ds(at, CHUNK), :] for ref in (pp, qq, rr))
        keep = 1.0 - relaxation
        return keep * s + (p * hs + q * hg), keep * g + (q * hs + r * hg)

    def sweep(f, new):
        def body(at):
            new[0, pl.ds(at + PITCH, CHUNK), :], new[1, pl.ds(at + PITCH, CHUNK), :] = relaxed(f, at)

        chunks(body)

    sweep(f0, f1)
    send_halo(1)

    def upstream(d):
        return jnp.full((cx, nz), place, jnp.int32) >= d

    for copy in group_copies(0, s_blk, s_rec):
        copy.wait()
    s_before = s_after = jnp.ones((cx, nz), jnp.float32)
    for d in range(1, group):
        s_d = s_rec[d - 1]
        s_before = jnp.where(upstream(d), s_before * s_d, s_before)
        s_after = jnp.where(upstream(d), s_after, s_after * s_d)
    s_pre[...] = s_before
    s_row[...] = s_before * s_blk[...] * s_after
    for sends, _, copy in row_copies(1, s_row, s_rrec):
        pl.when(sends)(copy.start)

    take_halo(1)
    sweep(f1, f2)
    send_halo(2)
    take_halo(2)

    def residual(at):
        s, g, hs, hg = beside(f2, at)
        k = c_f[pl.ds(at, CHUNK), :]
        gd = (gas_cap + flow_rate + gas_conduct * 2.0 * 2.25) + k
        res[0, pl.ds(at, CHUNK), :] = hs - (diag[pl.ds(at, CHUNK), :] * s - k * g)
        res[1, pl.ds(at, CHUNK), :] = hg - (gd * g - k * s)

    chunks(residual)

    state = jnp.zeros((cx, nz), jnp.float32)
    for j in range(cy):
        r_s = block_sum(lambda at: res[0, at, :], j)
        r_g = block_sum(lambda at: res[1, at, :], j)
        offset = (r_g + csum[j] * r_s * isol[j]) * iden[j]
        cres[j], offs[j] = r_s, offset
        state = slopes[j] * state + offset
    o_blk[...] = state
    for copy in group_copies(2, o_blk, o_rec):
        copy.start()
    for sends, receives, copy in row_copies(1, s_row, s_rrec):
        pl.when(sends)(copy.wait_send)
        pl.when(receives)(copy.wait_recv)
    for copy in group_copies(2, o_blk, o_rec):
        copy.wait()
    state = jnp.zeros((cx, nz), jnp.float32)
    for d in range(group - 1, 0, -1):
        state = jnp.where(upstream(d), s_rec[d - 1] * state + o_rec[d - 1], state)
    before = state
    state = s_blk[...] * state + o_blk[...]
    for d in range(group - 1, 0, -1):
        state = jnp.where(upstream(d), state, s_rec[d - 1] * state + o_rec[d - 1])
    o_row[...] = state
    for sends, _, copy in row_copies(3, o_row, o_rrec):
        pl.when(sends)(copy.start)
    for sends, receives, copy in row_copies(3, o_row, o_rrec):
        pl.when(sends)(copy.wait_send)
        pl.when(receives)(copy.wait_recv)
    state = jnp.zeros((cx, nz), jnp.float32)
    for d in range(n_group - 1, 0, -1):
        state = s_rrec[d - 1] * state + o_rrec[d - 1]
    error = s_pre[...] * state + before
    for j in range(cy):
        error = slopes[j] * error + offs[j]
        solid_error = (cres[j] + csum[j] * error) * isol[j]
        for a in (PITCH, 2 * PITCH):
            for b in (0, 1):
                at = pl.ds(2 * j + a + b, cx, stride=2 * PITCH)
                f3[0, at, :] = f2[0, at, :] + solid_error
                f3[1, at, :] = f2[1, at, :] + error

    send_halo(3)
    take_halo(3)
    sweep(f3, f4)
    send_halo(4)
    take_halo(4)

    def last(i, _):
        s, g = relaxed(f4, pl.multiple_of(i * CHUNK, CHUNK))
        n = CHUNK // PITCH
        for m in range(n):
            o_v[0, i * n + m] = s[m * PITCH:m * PITCH + ny]
            o_v[1, i * n + m] = g[m * PITCH:m * PITCH + ny]
        return 0

    lax.fori_loop(0, rows // CHUNK, last, 0)
    store = pltpu.make_async_copy(o_v, out, in_sem.at[0])
    store.start()
    store.wait()


def shards(n_gx, n_gy, temps, right_side, exchange, coupling):
    _, nx, ny, nz = temps.shape
    group = 8 if n_gy % 8 == 0 else 2
    n_group = n_gy // group
    rows, cx, cy = nx * PITCH, nx // 2, ny // 2
    f32 = jnp.float32
    padded = rows + 2 * PITCH
    kinds = max(group, n_group) - 1
    vmem = lambda *shape: pltpu.VMEM(shape, f32)
    line = lambda *lead: pltpu.VMEM((*lead, cx, nz), f32)
    scratch = [
        vmem(2, nx, ny, nz), vmem(2, nx, ny, nz), vmem(nx, ny, nz), vmem(nx, ny, nz), vmem(2, nx, ny, nz),
        vmem(3, padded, nz), vmem(2, padded, nz), vmem(2, padded, nz), vmem(2, padded, nz), vmem(2, padded, nz),
        vmem(2, rows, nz), vmem(rows, nz),
        vmem(rows + PITCH, nz), vmem(rows + 8, nz), vmem(rows, nz), vmem(rows, nz),
        vmem(rows, nz), vmem(rows, nz), vmem(rows, nz), vmem(2, rows, nz),
        vmem(STAGES, 2, 3, nx, nz), vmem(STAGES, 2, 3, nx, nz),
        line(cy), line(cy), line(cy), line(cy), line(cy), line(cy),
        line(), line(), line(group - 1), line(group - 1),
        line(), line(), line(n_group - 1), line(n_group - 1), line(),
        pltpu.SemaphoreType.DMA((4,)),
        pltpu.SemaphoreType.DMA((STAGES, 4)), pltpu.SemaphoreType.DMA((STAGES, 4)),
        pltpu.SemaphoreType.DMA((4, kinds)), pltpu.SemaphoreType.DMA((4, kinds)),
    ]
    return pl.pallas_call(
        functools.partial(kernel, (nx, ny, nz, n_gx, n_gy, group)),
        out_shape=jax.ShapeDtypeStruct(temps.shape, f32),
        in_specs=[pl.BlockSpec(memory_space=pl.ANY)] * 4,
        out_specs=pl.BlockSpec(memory_space=pl.ANY),
        scratch_shapes=scratch,
        compiler_params=pltpu.CompilerParams(collective_id=0, has_side_effects=True),
    )(temps, right_side, exchange, coupling)


def solution(mesh):
    return jax.shard_map(
        functools.partial(shards, mesh.shape["gx"], mesh.shape["gy"]),
        mesh=mesh,
        in_specs=(
            P(None, "gx", "gy", None),
            P(None, "gx", "gy", None),
            P("gx", "gy", None),
            P("gx", "gy", None),
        ),
        out_specs=P(None, "gx", "gy", None),
        check_vma=False,
    )
```

time: 272 us -> 52.9 us (0.19)
  the two profiles are of different devices: /device:TPU:247 before, /device:TPU:56 now
where the time goes in v1:
time: 52.9 us; the launch traced here: 52.6 us
  Pallas kernels  46 us (87%)
  local copies, waits for them, and re-layouts  6.6 us (12%)
    pallas_call x1, Pallas kernels, shards(): pl.pallas_call(functools.partial(kernel, (nx, ny, nz, n_gx, n_gy, group))...  46 us
    unnamed x10, local copies, waits for them, and re-layouts  4.69 us
    pallas_call x1, local copies, waits for them, and re-layouts, shards(): pl.pallas_call(functools.partial(kernel, (nx, ny, nz, n_gx, n_gy, group))...  1.91 us

profile of v1, /device:TPU:56, one launch (start us, length us, event | category | flops | bytes accessed | tf_op | source)
XLA Modules:
  0.0 52.6 jit_solution(9851460151560708219)
XLA Ops:
  0.0 0.0 copy-start.2
  0.0 0.0 copy-start
  0.0 1.8 %copy.7.exch = f32[32,12,128]{2,1,0:T(8,128)} copy(f32[32,12,128]{2,0,1:T(8,128)} %param.6) | data formatting | bytes 393216 | tf_op args[2]
  1.8 0.0 copy-done.2
  1.8 0.8 %copy.8.coup = f32[32,12,128]{2,1,0:T(8,128)} copy(f32[32,12,128]{2,0,1:T(8,128)S(1)} %copy-done.2) | data formatting | bytes 393216 | tf_op args[3]
  2.6 0.0 copy-done
  2.6 0.0 copy-start.1
  2.6 1.0 %copy.5.temps = f32[2,32,12,128]{3,2,1,0:T(8,128)} copy(f32[2,32,12,128]{3,1,2,0:T(8,128)S(1)} %copy-done) | data formatting | bytes 786432 | tf_op args[0]
  3.7 0.0 copy-done.1
  3.7 1.0 %copy.6.right = f32[2,32,12,128]{3,2,1,0:T(8,128)} copy(f32[2,32,12,128]{3,1,2,0:T(8,128)S(1)} %copy-done.1) | data formatting | bytes 786432 | tf_op args[1]
  4.7 46.0 %shard_map.46 = f32[2,32,12,128]{3,2,1,0:T(8,128)} custom-call(f32[2,32,12,128]{3,2,1,0:T(8,128)} %copy.5.temps, f32[2,32,12,128]{3,2,1,0:T(8,128)} %copy.6.right, f32[32,12,128]{2,1,0:T(8,128)} %copy.7.exch, f32[32,12,128]{2,1,0:T(8,128)} %copy.8.coup), custom_call_target="tpu_custom_call" | custom-call | tf_op jit(solution)/shard_map/pallas_call | solution.py:366
  50.7 1.9 %copy.9 = f32[2,32,12,128]{3,1,2,0:T(8,128)} copy(f32[2,32,12,128]{3,2,1,0:T(8,128)} %shard_map.46) | data formatting | bytes 786432 | tf_op jit(solution)/shard_map/pallas_call | solution.py:366
Async XLA Ops:
  0.0 1.8 %copy-start.2 = (f32[32,12,128]{2,0,1:T(8,128)S(1)}, f32[32,12,128]{2,0,1:T(8,128)}, u32[]{:S(2)}) copy-start(f32[32,12,128]{2,0,1:T(8,128)} %param.7) | copy-start | bytes 589828
  0.0 2.6 %copy-start = (f32[2,32,12,128]{3,1,2,0:T(8,128)S(1)}, f32[2,32,12,128]{3,1,2,0:T(8,128)}, u32[]{:S(2)}) copy-start(f32[2,32,12,128]{3,1,2,0:T(8,128)} %param.4) | copy-start | bytes 1179652
  2.6 1.0 %copy-start.1 = (f32[2,32,12,128]{3,1,2,0:T(8,128)S(1)}, f32[2,32,12,128]{3,1,2,0:T(8,128)}, u32[]{:S(2)}) copy-start(f32[2,32,12,128]{3,1,2,0:T(8,128)} %param.5) | copy-start | bytes 1179652

commit v2 on v1

v2 whole, which is shorter than its diff:
```python
import functools

import jax
import jax.numpy as jnp
from jax import lax
from jax.experimental import pallas as pl
from jax.experimental.pallas import tpu as pltpu
from jax.sharding import PartitionSpec as P

MESH = pl.DeviceIdType.MESH
EDGE = 8

solid_cap = 0.5
gas_cap = 0.02
flow_rate = 40.0
gas_conduct = 0.05
relaxation = 0.8
lump_factor = 0.25
STAGES = 5


def kernel(dims, temps, right, exch, coup, out, *scratch):
    nx, ny, nz, n_gx, n_gy, group = dims
    pitch = nx + EDGE
    cx, cy = nx // 2, ny // 2
    n_group = n_gy // group
    (e_in, b_f, c_f, o_v, f0, f1, f2, f3, f4, fx, fy, fz, diag, pp, qq, rr, res,
     xs, xr, slopes, csum, isol, iden, cres, offs, s_blk, o_blk, s_rec, o_rec, s_row, o_row, s_rrec, o_rrec, s_pre,
     in_sem, h_send, h_recv, g_send, g_recv) = scratch
    ix, iy = lax.axis_index("gx"), lax.axis_index("gy")
    place, row = lax.rem(iy, group), lax.div(iy, group)

    loads = [
        pltpu.make_async_copy(temps.at[:, pl.ds(y * nx, nx)], f0.at[0:2, pl.ds((y + 1) * pitch, nx)], in_sem.at[3 + y])
        for y in range(ny)
    ]
    loads.append(pltpu.make_async_copy(exch, e_in, in_sem.at[0]))
    more = [pltpu.make_async_copy(coup, c_f, in_sem.at[1]), pltpu.make_async_copy(right, b_f, in_sem.at[2])]
    for load in loads + more:
        load.start()

    barrier = pltpu.get_barrier_semaphore()

    def greet(gx, gy):
        pl.semaphore_signal(barrier, inc=1, device_id=(gx, gy), device_id_type=MESH)

    for d in range(1, group):
        greet(ix, row * group + lax.rem(place + d, group))
    for d in range(1, n_group):
        greet(ix, lax.rem(row + d, n_group) * group + place)
    up_y, down_y, up_x, down_x = iy < n_gy - 1, iy > 0, ix < n_gx - 1, ix > 0
    pl.when(up_y)(lambda: greet(ix, iy + 1))
    pl.when(down_y)(lambda: greet(ix, iy - 1))
    pl.when(up_x)(lambda: greet(ix + 1, iy))
    pl.when(down_x)(lambda: greet(ix - 1, iy))

    fields = (f0, f1, f2, f3, f4)
    plane_zero = jnp.zeros((nx, nz), jnp.float32)
    side_zero = jnp.zeros((ny, nz), jnp.float32)

    def clear_planes(at):
        for f in fields:
            for n in range(f.shape[0]):
                f[n, at:at + nx, :] = plane_zero

    def clear_sides(side):
        for st in range(STAGES):
            for n in range(3 if st == 0 else 2):
                xr[st, side, n] = side_zero

    pl.when(jnp.logical_not(down_y))(lambda: clear_planes(0))
    pl.when(jnp.logical_not(up_y))(lambda: clear_planes((ny + 1) * pitch))
    pl.when(jnp.logical_not(down_x))(lambda: clear_sides(0))
    pl.when(jnp.logical_not(up_x))(lambda: clear_sides(1))
    for d in range(1, n_group):

        @pl.when(row < d)
        def _():
            s_rrec[d - 1] = jnp.ones((cx, nz), jnp.float32)
            o_rrec[d - 1] = jnp.zeros((cx, nz), jnp.float32)

    def halo_copies(st):
        f = fields[st]
        nf = f.shape[0]
        plane = lambda y: f.at[:, (y + 1) * pitch:(y + 1) * pitch + nx]
        parts = (
            (up_y, down_y, plane(ny - 1), plane(-1), (ix, iy + 1)),
            (down_y, up_y, plane(0), plane(ny), (ix, iy - 1)),
            (up_x, down_x, xs.at[st, 1, :nf], xr.at[st, 0, :nf], (ix + 1, iy)),
            (down_x, up_x, xs.at[st, 0, :nf], xr.at[st, 1, :nf], (ix - 1, iy)),
        )
        return [
            (sends, receives, pltpu.make_async_remote_copy(
                src_ref=src, dst_ref=dst, send_sem=h_send.at[st, i], recv_sem=h_recv.at[st, i],
                device_id=to, device_id_type=MESH))
            for i, (sends, receives, src, dst, to) in enumerate(parts)
        ]

    def send_halo(st):
        f = fields[st]
        for n in range(f.shape[0]):
            xs[st, 0, n] = f[n, pl.ds(pitch, ny, stride=pitch), :]
            xs[st, 1, n] = f[n, pl.ds(pitch + nx - 1, ny, stride=pitch), :]
        for sends, _, copy in halo_copies(st):
            pl.when(sends)(copy.start)

    def take_halo(st):
        f = fields[st]
        for sends, receives, copy in halo_copies(st):
            pl.when(sends)(copy.wait_send)
            pl.when(receives)(copy.wait_recv)
        for n in range(f.shape[0]):
            f[n, pl.ds(pitch - 1, ny, stride=pitch), :] = xr[st, 0, n]
            f[n, pl.ds(pitch + nx, ny, stride=pitch), :] = xr[st, 1, n]

    def group_copies(kind, block, received):
        return [
            pltpu.make_async_remote_copy(
                src_ref=block, dst_ref=received.at[d - 1],
                send_sem=g_send.at[kind, d - 1], recv_sem=g_recv.at[kind, d - 1],
                device_id=(ix, row * group + lax.rem(place + d, group)), device_id_type=MESH)
            for d in range(1, group)
        ]

    def row_copies(kind, block, received):
        return [
            (row + d < n_group, row >= d, pltpu.make_async_remote_copy(
                src_ref=block, dst_ref=received.at[d - 1],
                send_sem=g_send.at[kind, d - 1], recv_sem=g_recv.at[kind, d - 1],
                device_id=(ix, (row + d) * group + place), device_id_type=MESH))
            for d in range(1, n_group)
        ]

    def planes(body, unroll=2):
        def step(y, _):
            body(y, pl.multiple_of(y * nx, 8), pl.multiple_of((y + 1) * pitch, 8))
            return 0

        lax.fori_loop(0, ny, step, 0, unroll=unroll)

    def conductivity(y, at, on):
        t = f0[0, pl.ds(on, nx), :]
        f0[2, pl.ds(on, nx), :] = 1.0 + 4.0 * e_in[pl.ds(at, nx), :] * (t * t * t)

    for load in loads:
        load.wait()
    planes(conductivity)
    n_halo = sum(v.astype(jnp.int32) for v in (up_y, down_y, up_x, down_x))
    pl.semaphore_wait(barrier, (group - 1) + (n_group - 1) + n_halo)
    send_halo(0)
    for load in more:
        load.wait()

    def block_sum(load, j, step):
        total = None
        for a in (0, step):
            for b in (0, 1):
                part = load(pl.ds(2 * j * step + a + b, cx, stride=2))
                total = part if total is None else total + part
        return total

    s_all = None
    for j in range(cy):
        cs = block_sum(lambda at: c_f[at, :], j, nx)
        cond = block_sum(lambda at: f0[2, pl.ds(at.start + pitch, at.size, stride=at.stride), :], j, pitch)
        inv_solid = 1.0 / (4.0 * solid_cap + cs + lump_factor * cond)
        inv_denom = 1.0 / (4.0 * gas_cap + cs + 2.0 * flow_rate - cs * cs * inv_solid)
        slope = 2.0 * flow_rate * inv_denom
        csum[j], isol[j], iden[j], slopes[j] = cs, inv_solid, inv_denom, slope
        s_all = slope if s_all is None else s_all * slope
    s_blk[...] = s_all
    for copy in group_copies(0, s_blk, s_rec):
        copy.start()

    take_halo(0)

    lane = lax.broadcasted_iota(jnp.int32, (nx, nz), 1)
    not_last, not_first = lane < nz - 1, lane > 0
    gas_zp = jnp.where(not_last, gas_conduct * 0.25, 0.0)
    gas_zm = jnp.where(not_first, gas_conduct * 0.25, 0.0)
    fy[0:nx] = 0.5 * (f0[2, 0:nx, :] + f0[2, pitch:pitch + nx, :])

    def set_up(y, at, on):
        c = f0[2, pl.ds(on, nx), :]
        xp = 0.5 * (c + f0[2, pl.ds(on + 1, nx), :])
        xm = 0.5 * (c + f0[2, pl.ds(on - 1, nx), :])
        yp = 0.5 * (c + f0[2, pl.ds(on + pitch, nx), :])
        ym = 0.5 * (c + f0[2, pl.ds(on - pitch, nx), :])
        zp = 0.125 * (c + jnp.where(not_last, pltpu.roll(c, nz - 1, 1), 0.0))
        zm = 0.125 * (c + jnp.where(not_first, pltpu.roll(c, 1, 1), 0.0))
        fx[pl.ds(on, nx), :] = xp
        fx[pl.ds(on - 8, 8), :] = 0.5 * (f0[2, pl.ds(on - 8, 8), :] + f0[2, pl.ds(on - 7, 8), :])
        fy[pl.ds(at + nx, nx), :] = yp
        fz[pl.ds(at, nx), :] = jnp.where(not_last, zp, 0.0)
        k = c_f[pl.ds(at, nx), :]
        sd = solid_cap + k + (((xp + xm) + (yp + ym)) + (zp + zm))
        gd = (gas_cap + flow_rate + gas_conduct * 2.0 * 2.25) + k
        w = relaxation / (sd * gd - k * k)
        diag[pl.ds(at, nx), :] = sd
        pp[pl.ds(at, nx), :] = gd * w
        qq[pl.ds(at, nx), :] = k * w
        rr[pl.ds(at, nx), :] = sd * w

    planes(set_up)

    def beside(f, at, on):
        s = f[0, pl.ds(on, nx), :]
        g = f[1, pl.ds(on, nx), :]
        z = fz[pl.ds(at, nx), :]
        hs = b_f[0, pl.ds(at, nx), :]
        hs += fy[pl.ds(at + nx, nx), :] * f[0, pl.ds(on + pitch, nx), :]
        hs += fy[pl.ds(at, nx), :] * f[0, pl.ds(on - pitch, nx), :]
        hs += fx[pl.ds(on, nx), :] * f[0, pl.ds(on + 1, nx), :]
        hs += fx[pl.ds(on - 1, nx), :] * f[0, pl.ds(on - 1, nx), :]
        hs += z * pltpu.roll(s, nz - 1, 1) + pltpu.roll(z * s, 1, 1)
        hg = b_f[1, pl.ds(at, nx), :]
        hg += (flow_rate + gas_conduct) * f[1, pl.ds(on - pitch, nx), :]
        hg += gas_conduct * (
            f[1, pl.ds(on + pitch, nx), :]
            + (f[1, pl.ds(on - 1, nx), :] + f[1, pl.ds(on + 1, nx), :]))
        hg += gas_zp * pltpu.roll(g, nz - 1, 1) + gas_zm * pltpu.roll(g, 1, 1)
        return s, g, hs, hg

    def relaxed(f, at, on):
        s, g, hs, hg = beside(f, at, on)
        p, q, r = (ref[pl.ds(at, nx), :] for ref in (pp, qq, rr))
        keep = 1.0 - relaxation
        return keep * s + (p * hs + q * hg), keep * g + (q * hs + r * hg)

    def sweep(f, new):
        def body(y, at, on):
            new[0, pl.ds(on, nx), :], new[1, pl.ds(on, nx), :] = relaxed(f, at, on)

        planes(body)

    sweep(f0, f1)
    send_halo(1)

    def upstream(d):
        return jnp.full((cx, nz), place, jnp.int32) >= d

    for copy in group_copies(0, s_blk, s_rec):
        copy.wait()
    s_before = s_after = jnp.ones((cx, nz), jnp.float32)
    for d in range(1, group):
        s_d = s_rec[d - 1]
        s_before = jnp.where(upstream(d), s_before * s_d, s_before)
        s_after = jnp.where(upstream(d), s_after, s_after * s_d)
    s_pre[...] = s_before
    s_row[...] = s_before * s_blk[...] * s_after
    for sends, _, copy in row_copies(1, s_row, s_rrec):
        pl.when(sends)(copy.start)

    take_halo(1)
    sweep(f1, f2)
    send_halo(2)
    take_halo(2)

    def residual(y, at, on):
        s, g, hs, hg = beside(f2, at, on)
        k = c_f[pl.ds(at, nx), :]
        gd = (gas_cap + flow_rate + gas_conduct * 2.0 * 2.25) + k
        res[0, pl.ds(at, nx), :] = hs - (diag[pl.ds(at, nx), :] * s - k * g)
        res[1, pl.ds(at, nx), :] = hg - (gd * g - k * s)

    planes(residual)

    state = jnp.zeros((cx, nz), jnp.float32)
    for j in range(cy):
        r_s = block_sum(lambda at: res[0, at, :], j, nx)
        r_g = block_sum(lambda at: res[1, at, :], j, nx)
        offset = (r_g + csum[j] * r_s * isol[j]) * iden[j]
        cres[j], offs[j] = r_s, offset
        state = slopes[j] * state + offset
    o_blk[...] = state
    for copy in group_copies(2, o_blk, o_rec):
        copy.start()
    for sends, receives, copy in row_copies(1, s_row, s_rrec):
        pl.when(sends)(copy.wait_send)
        pl.when(receives)(copy.wait_recv)
    for copy in group_copies(2, o_blk, o_rec):
        copy.wait()
    state = jnp.zeros((cx, nz), jnp.float32)
    for d in range(group - 1, 0, -1):
        state = jnp.where(upstream(d), s_rec[d - 1] * state + o_rec[d - 1], state)
    before = state
    state = s_blk[...] * state + o_blk[...]
    for d in range(group - 1, 0, -1):
        state = jnp.where(upstream(d), state, s_rec[d - 1] * state + o_rec[d - 1])
    o_row[...] = state
    for sends, _, copy in row_copies(3, o_row, o_rrec):
        pl.when(sends)(copy.start)
    for sends, receives, copy in row_copies(3, o_row, o_rrec):
        pl.when(sends)(copy.wait_send)
        pl.when(receives)(copy.wait_recv)
    state = jnp.zeros((cx, nz), jnp.float32)
    for d in range(n_group - 1, 0, -1):
        state = s_rrec[d - 1] * state + o_rrec[d - 1]
    error = s_pre[...] * state + before
    for j in range(cy):
        error = slopes[j] * error + offs[j]
        solid_error = (cres[j] + csum[j] * error) * isol[j]
        for a in (pitch, 2 * pitch):
            for b in (0, 1):
                at = pl.ds(2 * j * pitch + a + b, cx, stride=2)
                f3[0, at, :] = f2[0, at, :] + solid_error
                f3[1, at, :] = f2[1, at, :] + error

    send_halo(3)
    take_halo(3)
    sweep(f3, f4)
    send_halo(4)
    take_halo(4)

    def last(y, at, on):
        o_v[0, pl.ds(at, nx), :], o_v[1, pl.ds(at, nx), :] = relaxed(f4, at, on)

    planes(last)
    store = pltpu.make_async_copy(o_v, out, in_sem.at[0])
    store.start()
    store.wait()


def shards(n_gx, n_gy, temps, right_side, exchange, coupling):
    _, nx, ny, nz = temps.shape
    group = 8 if n_gy % 8 == 0 else 2
    n_group = n_gy // group
    rows, cx, cy = nx * ny, nx // 2, ny // 2
    f32 = jnp.float32
    padded = (nx + EDGE) * (ny + 2)
    kinds = max(group, n_group) - 1
    vmem = lambda *shape: pltpu.VMEM(shape, f32)
    line = lambda *lead: pltpu.VMEM((*lead, cx, nz), f32)
    scratch = [
        vmem(rows, nz), vmem(2, rows, nz), vmem(rows, nz), vmem(2, rows, nz),
        vmem(3, padded, nz), vmem(2, padded, nz), vmem(2, padded, nz), vmem(2, padded, nz), vmem(2, padded, nz),
        vmem(padded, nz), vmem(rows + nx, nz), vmem(rows, nz), vmem(rows, nz),
        vmem(rows, nz), vmem(rows, nz), vmem(rows, nz), vmem(2, rows, nz),
        vmem(STAGES, 2, 3, ny, nz), vmem(STAGES, 2, 3, ny, nz),
        line(cy), line(cy), line(cy), line(cy), line(cy), line(cy),
        line(), line(), line(group - 1), line(group - 1),
        line(), line(), line(n_group - 1), line(n_group - 1), line(),
        pltpu.SemaphoreType.DMA((3 + ny,)),
        pltpu.SemaphoreType.DMA((STAGES, 4)), pltpu.SemaphoreType.DMA((STAGES, 4)),
        pltpu.SemaphoreType.DMA((4, kinds)), pltpu.SemaphoreType.DMA((4, kinds)),
    ]
    flat = lambda a: jnp.swapaxes(a, -3, -2).reshape(*a.shape[:-3], rows, nz)
    out = pl.pallas_call(
        functools.partial(kernel, (nx, ny, nz, n_gx, n_gy, group)),
        out_shape=jax.ShapeDtypeStruct((2, rows, nz), f32),
        in_specs=[pl.BlockSpec(memory_space=pl.ANY)] * 4,
        out_specs=pl.BlockSpec(memory_space=pl.ANY),
        scratch_shapes=scratch,
        compiler_params=pltpu.CompilerParams(collective_id=0, has_side_effects=True),
    )(flat(temps), flat(right_side), flat(exchange), flat(coupling))
    return jnp.swapaxes(out.reshape(2, ny, nx, nz), 1, 2)


def solution(mesh):
    return jax.shard_map(
        functools.partial(shards, mesh.shape["gx"], mesh.shape["gy"]),
        mesh=mesh,
        in_specs=(
            P(None, "gx", "gy", None),
            P(None, "gx", "gy", None),
            P("gx", "gy", None),
            P("gx", "gy", None),
        ),
        out_specs=P(None, "gx", "gy", None),
        check_vma=False,
    )
```

time: 52.9 us -> 46 us (0.87)
  local copies, waits for them, and re-layouts: 6.6 us -> 1.77 us
  Pallas kernels: 46 us -> 44 us
    unnamed x10 -> x1, local copies, waits for them, and re-layouts: 4.69 us -> 1.77 us
    pallas_call x1, Pallas kernels: 46 us -> 44 us  [shards(): pl.pallas_call(functools.partial(kernel, (nx, ny, nz, n_gx, n_gy, group))...]
    pallas_call x1 -> x0, local copies, waits for them, and re-layouts: 1.91 us -> none  [shards(): pl.pallas_call(functools.partial(kernel, (nx, ny, nz, n_gx, n_gy, group))...]
where the time goes in v2:
time: 46 us; the launch traced here: 45.8 us
  Pallas kernels  44 us (96%)
  local copies, waits for them, and re-layouts  1.77 us (4%)
    pallas_call x1, Pallas kernels, shards(): pl.pallas_call(functools.partial(kernel, (nx, ny, nz, n_gx, n_gy, group))...  44 us
    unnamed x1, local copies, waits for them, and re-layouts  1.77 us

profile of v2, /device:TPU:56, one launch (start us, length us, event | category | flops | bytes accessed | tf_op | source)
XLA Modules:
  0.0 45.8 jit_solution(1195493174840850595)
XLA Ops:
  0.0 44.0 %shard_map.46 = f32[2,384,128]{2,1,0:T(8,128)} custom-call(f32[2,384,128]{2,1,0:T(8,128)} %bitcast.16, f32[2,384,128]{2,1,0:T(8,128)} %bitcast.17, f32[384,128]{1,0:T(8,128)} %bitcast.18, f32[384,128]{1,0:T(8,128)} %bitcast.19), custom_call_target="tpu_custom_call" | custom-call | tf_op jit(solution)/shard_map/pallas_call | solution.py:348
  44.1 1.8 %copy.6 = f32[2,32,12,128]{3,1,2,0:T(8,128)} copy(f32[2,32,12,128]{3,1,2,0:T(8,128)} %bitcast.15) | data formatting | bytes 786432

commit v3 on v2

--- a/solution.py
+++ b/solution.py
@@ -17,6 +17,17 @@
 relaxation = 0.8
 lump_factor = 0.25
 STAGES = 5
+
+
+class Cells:
+    def __init__(self, at, on, n, step=None, skip=None):
+        self.at, self.on, self.n, self.step, self.skip = at, on, n, step, skip
+
+    def coef(self, shift=0):
+        return pl.ds(self.at + shift, self.n, stride=self.step)
+
+    def field(self, shift=0):
+        return pl.ds(self.on + shift, self.n, stride=self.skip)
 
 
 def kernel(dims, temps, right, exch, coup, out, *scratch):
@@ -131,20 +142,29 @@
             for d in range(1, n_group)
         ]
 
-    def planes(body, unroll=2):
+    def plane(y):
+        return Cells(y * nx, (y + 1) * pitch, nx)
+
+    def inner(body, low=1, high=ny - 1, unroll=2):
         def step(y, _):
-            body(y, pl.multiple_of(y * nx, 8), pl.multiple_of((y + 1) * pitch, 8))
+            body(Cells(pl.multiple_of(y * nx, 8), pl.multiple_of((y + 1) * pitch, 8), nx))
             return 0
 
-        lax.fori_loop(0, ny, step, 0, unroll=unroll)
-
-    def conductivity(y, at, on):
-        t = f0[0, pl.ds(on, nx), :]
-        f0[2, pl.ds(on, nx), :] = 1.0 + 4.0 * e_in[pl.ds(at, nx), :] * (t * t * t)
+        lax.fori_loop(low, high, step, 0, unroll=unroll)
+
+    def outer(body):
+        for y in (0, ny - 1):
+            body(plane(y))
+        for x in (0, nx - 1):
+            body(Cells(x, pitch + x, ny, nx, pitch))
+
+    def conductivity(u):
+        t = f0[0, u.field(), :]
+        f0[2, u.field(), :] = 1.0 + 4.0 * e_in[u.coef(), :] * (t * t * t)
 
     for load in loads:
         load.wait()
-    planes(conductivity)
+    inner(conductivity, 0, ny)
     n_halo = sum(v.astype(jnp.int32) for v in (up_y, down_y, up_x, down_x))
     pl.semaphore_wait(barrier, (group - 1) + (n_group - 1) + n_halo)
     send_halo(0)
@@ -172,69 +192,72 @@
     for copy in group_copies(0, s_blk, s_rec):
         copy.start()
 
-    take_halo(0)
-
-    lane = lax.broadcasted_iota(jnp.int32, (nx, nz), 1)
-    not_last, not_first = lane < nz - 1, lane > 0
-    gas_zp = jnp.where(not_last, gas_conduct * 0.25, 0.0)
-    gas_zm = jnp.where(not_first, gas_conduct * 0.25, 0.0)
-    fy[0:nx] = 0.5 * (f0[2, 0:nx, :] + f0[2, pitch:pitch + nx, :])
-
-    def set_up(y, at, on):
-        c = f0[2, pl.ds(on, nx), :]
-        xp = 0.5 * (c + f0[2, pl.ds(on + 1, nx), :])
-        xm = 0.5 * (c + f0[2, pl.ds(on - 1, nx), :])
-        yp = 0.5 * (c + f0[2, pl.ds(on + pitch, nx), :])
-        ym = 0.5 * (c + f0[2, pl.ds(on - pitch, nx), :])
-        zp = 0.125 * (c + jnp.where(not_last, pltpu.roll(c, nz - 1, 1), 0.0))
-        zm = 0.125 * (c + jnp.where(not_first, pltpu.roll(c, 1, 1), 0.0))
-        fx[pl.ds(on, nx), :] = xp
-        fx[pl.ds(on - 8, 8), :] = 0.5 * (f0[2, pl.ds(on - 8, 8), :] + f0[2, pl.ds(on - 7, 8), :])
-        fy[pl.ds(at + nx, nx), :] = yp
-        fz[pl.ds(at, nx), :] = jnp.where(not_last, zp, 0.0)
-        k = c_f[pl.ds(at, nx), :]
+    lane = lax.broadcasted_iota(jnp.int32, (1, nz), 1)
+    not_last = (lane < nz - 1).astype(jnp.float32)
+    not_first = (lane > 0).astype(jnp.float32)
+    gas_zp = gas_conduct * 0.25 * not_last
+    gas_zm = gas_conduct * 0.25 * not_first
+
+    def set_up(u):
+        c = f0[2, u.field(), :]
+        xp = 0.5 * (c + f0[2, u.field(1), :])
+        xm = 0.5 * (c + f0[2, u.field(-1), :])
+        yp = 0.5 * (c + f0[2, u.field(pitch), :])
+        ym = 0.5 * (c + f0[2, u.field(-pitch), :])
+        zp = 0.125 * (c + not_last * pltpu.roll(c, nz - 1, 1))
+        zm = 0.125 * (c + not_first * pltpu.roll(c, 1, 1))
+        fx[u.field(), :] = xp
+        if u.step is None:
+            fx[pl.ds(u.on - 8, 8), :] = 0.5 * (f0[2, pl.ds(u.on - 8, 8), :] + f0[2, pl.ds(u.on - 7, 8), :])
+        else:
+            fx[u.field(-1), :] = xm
+        fy[u.coef(), :] = ym
+        fy[u.coef(nx), :] = yp
+        fz[u.coef(), :] = not_last * zp
+        k = c_f[u.coef(), :]
         sd = solid_cap + k + (((xp + xm) + (yp + ym)) + (zp + zm))
         gd = (gas_cap + flow_rate + gas_conduct * 2.0 * 2.25) + k
         w = relaxation / (sd * gd - k * k)
-        diag[pl.ds(at, nx), :] = sd
-        pp[pl.ds(at, nx), :] = gd * w
-        qq[pl.ds(at, nx), :] = k * w
-        rr[pl.ds(at, nx), :] = sd * w
-
-    planes(set_up)
-
-    def beside(f, at, on):
-        s = f[0, pl.ds(on, nx), :]
-        g = f[1, pl.ds(on, nx), :]
-        z = fz[pl.ds(at, nx), :]
-        hs = b_f[0, pl.ds(at, nx), :]
-        hs += fy[pl.ds(at + nx, nx), :] * f[0, pl.ds(on + pitch, nx), :]
-        hs += fy[pl.ds(at, nx), :] * f[0, pl.ds(on - pitch, nx), :]
-        hs += fx[pl.ds(on, nx), :] * f[0, pl.ds(on + 1, nx), :]
-        hs += fx[pl.ds(on - 1, nx), :] * f[0, pl.ds(on - 1, nx), :]
+        diag[u.coef(), :] = sd
+        pp[u.coef(), :] = gd * w
+        qq[u.coef(), :] = k * w
+        rr[u.coef(), :] = sd * w
+
+    def beside(f, u):
+        s = f[0, u.field(), :]
+        g = f[1, u.field(), :]
+        z = fz[u.coef(), :]
+        hs = b_f[0, u.coef(), :]
+        hs += fy[u.coef(nx), :] * f[0, u.field(pitch), :]
+        hs += fy[u.coef(), :] * f[0, u.field(-pitch), :]
+        hs += fx[u.field(), :] * f[0, u.field(1), :]
+        hs += fx[u.field(-1), :] * f[0, u.field(-1), :]
         hs += z * pltpu.roll(s, nz - 1, 1) + pltpu.roll(z * s, 1, 1)
-        hg = b_f[1, pl.ds(at, nx), :]
-        hg += (flow_rate + gas_conduct) * f[1, pl.ds(on - pitch, nx), :]
-        hg += gas_conduct * (
-            f[1, pl.ds(on + pitch, nx), :]
-            + (f[1, pl.ds(on - 1, nx), :] + f[1, pl.ds(on + 1, nx), :]))
+        hg = b_f[1, u.coef(), :]
+        hg += (flow_rate + gas_conduct) * f[1, u.field(-pitch), :]
+        hg += gas_conduct * (f[1, u.field(pitch), :] + (f[1, u.field(-1), :] + f[1, u.field(1), :]))
         hg += gas_zp * pltpu.roll(g, nz - 1, 1) + gas_zm * pltpu.roll(g, 1, 1)
         return s, g, hs, hg
 
-    def relaxed(f, at, on):
-        s, g, hs, hg = beside(f, at, on)
-        p, q, r = (ref[pl.ds(at, nx), :] for ref in (pp, qq, rr))
+    def relaxed(f, u):
+        s, g, hs, hg = beside(f, u)
+        p, q, r = pp[u.coef(), :], qq[u.coef(), :], rr[u.coef(), :]
         keep = 1.0 - relaxation
         return keep * s + (p * hs + q * hg), keep * g + (q * hs + r * hg)
 
     def sweep(f, new):
-        def body(y, at, on):
-            new[0, pl.ds(on, nx), :], new[1, pl.ds(on, nx), :] = relaxed(f, at, on)
-
-        planes(body)
-
-    sweep(f0, f1)
+        def body(u):
+            new[0, u.field(), :], new[1, u.field(), :] = relaxed(f, u)
+
+        return body
+
+    inner(set_up)
+    inner(sweep(f0, f1))
+    take_halo(0)
+    outer(set_up)
+    outer(sweep(f0, f1))
     send_halo(1)
+    inner(sweep(f1, f2))
 
     def upstream(d):
         return jnp.full((cx, nz), place, jnp.int32) >= d
@@ -252,18 +275,19 @@
         pl.when(sends)(copy.start)
 
     take_halo(1)
-    sweep(f1, f2)
+    outer(sweep(f1, f2))
     send_halo(2)
+
+    def residual(u):
+        s, g, hs, hg = beside(f2, u)
+        k = c_f[u.coef(), :]
+        gd = (gas_cap + flow_rate + gas_conduct * 2.0 * 2.25) + k
+        res[0, u.coef(), :] = hs - (diag[u.coef(), :] * s - k * g)
+        res[1, u.coef(), :] = hg - (gd * g - k * s)
+
+    inner(residual)
     take_halo(2)
-
-    def residual(y, at, on):
-        s, g, hs, hg = beside(f2, at, on)
-        k = c_f[pl.ds(at, nx), :]
-        gd = (gas_cap + flow_rate + gas_conduct * 2.0 * 2.25) + k
-        res[0, pl.ds(at, nx), :] = hs - (diag[pl.ds(at, nx), :] * s - k * g)
-        res[1, pl.ds(at, nx), :] = hg - (gd * g - k * s)
-
-    planes(residual)
+    outer(residual)
 
     state = jnp.zeros((cx, nz), jnp.float32)
     for j in range(cy):
@@ -306,16 +330,17 @@
                 f3[0, at, :] = f2[0, at, :] + solid_error
                 f3[1, at, :] = f2[1, at, :] + error
 
+    def last(u):
+        o_v[0, u.coef(), :], o_v[1, u.coef(), :] = relaxed(f4, u)
+
     send_halo(3)
+    inner(sweep(f3, f4))
     take_halo(3)
-    sweep(f3, f4)
+    outer(sweep(f3, f4))
     send_halo(4)
+    inner(last)
     take_halo(4)
-
-    def last(y, at, on):
-        o_v[0, pl.ds(at, nx), :], o_v[1, pl.ds(at, nx), :] = relaxed(f4, at, on)
-
-    planes(last)
+    outer(last)
     store = pltpu.make_async_copy(o_v, out, in_sem.at[0])
     store.start()
     store.wait()

time: 46 us -> 42.9 us (0.933)
  Pallas kernels: 44 us -> 41 us
    pallas_call x1, Pallas kernels: 44 us -> 41 us  [shards(): pl.pallas_call(functools.partial(kernel, (nx, ny, nz, n_gx, n_gy, group))...]
where the time goes in v3:
time: 42.9 us; the launch traced here: 42.8 us
  Pallas kernels  41 us (96%)
  local copies, waits for them, and re-layouts  1.77 us (4%)
    pallas_call x1, Pallas kernels, shards(): pl.pallas_call(functools.partial(kernel, (nx, ny, nz, n_gx, n_gy, group))...  41 us
    unnamed x1, local copies, waits for them, and re-layouts  1.77 us

profile of v3, /device:TPU:56, one launch (start us, length us, event | category | flops | bytes accessed | tf_op | source)
XLA Modules:
  0.0 42.8 jit_solution(9816630671823584674)
XLA Ops:
  0.0 41.0 %shard_map.46 = f32[2,384,128]{2,1,0:T(8,128)} custom-call(f32[2,384,128]{2,1,0:T(8,128)} %bitcast.16, f32[2,384,128]{2,1,0:T(8,128)} %bitcast.17, f32[384,128]{1,0:T(8,128)} %bitcast.18, f32[384,128]{1,0:T(8,128)} %bitcast.19), custom_call_target="tpu_custom_call" | custom-call | tf_op jit(solution)/shard_map/pallas_call | solution.py:373
  41.0 1.8 %copy.6 = f32[2,32,12,128]{3,1,2,0:T(8,128)} copy(f32[2,32,12,128]{3,1,2,0:T(8,128)} %bitcast.15) | data formatting | bytes 786432

commit v4 on v3

--- a/solution.py
+++ b/solution.py
@@ -35,18 +35,22 @@
     pitch = nx + EDGE
     cx, cy = nx // 2, ny // 2
     n_group = n_gy // group
-    (e_in, b_f, c_f, o_v, f0, f1, f2, f3, f4, fx, fy, fz, diag, pp, qq, rr, res,
-     xs, xr, slopes, csum, isol, iden, cres, offs, s_blk, o_blk, s_rec, o_rec, s_row, o_row, s_rrec, o_rrec, s_pre,
-     in_sem, h_send, h_recv, g_send, g_recv) = scratch
+    (e_in, c_f, o_v, f0, f1, f2, f3, f4, cf, fx, fy, diag, res, xs, xr, xs3, xr3, coarse,
+     s_blk, o_blk, s_rec, o_rec, s_row, o_row, s_rrec, o_rrec, s_pre,
+     in_sem, h_send, h_recv, w_send, w_recv, g_send, g_recv) = scratch
+    P_, Q_, R_, FZ, B_S, B_G = range(6)
+    CSUM, ISOL, CRES, SLOPE, OFFS = range(5)
+    own = slice(nx, (ny + 1) * nx)
+    first_on = 2 * pitch
     ix, iy = lax.axis_index("gx"), lax.axis_index("gy")
     place, row = lax.rem(iy, group), lax.div(iy, group)
 
     loads = [
-        pltpu.make_async_copy(temps.at[:, pl.ds(y * nx, nx)], f0.at[0:2, pl.ds((y + 1) * pitch, nx)], in_sem.at[3 + y])
+        pltpu.make_async_copy(temps.at[:, pl.ds(y * nx, nx)], f0.at[0:2, pl.ds((y + 2) * pitch, nx)], in_sem.at[3 + y])
         for y in range(ny)
     ]
-    loads.append(pltpu.make_async_copy(exch, e_in, in_sem.at[0]))
-    more = [pltpu.make_async_copy(coup, c_f, in_sem.at[1]), pltpu.make_async_copy(right, b_f, in_sem.at[2])]
+    loads.append(pltpu.make_async_copy(exch, e_in.at[own], in_sem.at[0]))
+    more = [pltpu.make_async_copy(coup, c_f.at[own], in_sem.at[1]), pltpu.make_async_copy(right, cf.at[B_S:B_G + 1, own], in_sem.at[2])]
     for load in loads + more:
         load.start()
 
@@ -69,18 +73,28 @@
     plane_zero = jnp.zeros((nx, nz), jnp.float32)
     side_zero = jnp.zeros((ny, nz), jnp.float32)
 
-    def clear_planes(at):
+    def clear_planes(y, far, face, line):
         for f in fields:
             for n in range(f.shape[0]):
-                f[n, at:at + nx, :] = plane_zero
+                f[n, (y + 2) * pitch:(y + 2) * pitch + nx, :] = plane_zero
+        for n in range(2):
+            f2[n, (far + 2) * pitch:(far + 2) * pitch + nx, :] = plane_zero
+        for n in range(6):
+            cf[n, (y + 1) * nx:(y + 2) * nx, :] = plane_zero
+        fx[(y + 2) * pitch - 8:(y + 2) * pitch + nx, :] = jnp.zeros((nx + 8, nz), jnp.float32)
+        fy[face * nx:(face + 1) * nx, :] = plane_zero
+        for n in range(5):
+            coarse[n, line] = jnp.zeros((cx, nz), jnp.float32)
 
     def clear_sides(side):
         for st in range(STAGES):
             for n in range(3 if st == 0 else 2):
                 xr[st, side, n] = side_zero
-
-    pl.when(jnp.logical_not(down_y))(lambda: clear_planes(0))
-    pl.when(jnp.logical_not(up_y))(lambda: clear_planes((ny + 1) * pitch))
+        for n in range(2):
+            xr3[side, n] = jnp.zeros((ny + 2, nz), jnp.float32)
+
+    pl.when(jnp.logical_not(down_y))(lambda: clear_planes(-1, -2, 0, 0))
+    pl.when(jnp.logical_not(up_y))(lambda: clear_planes(ny, ny + 1, ny + 2, cy + 1))
     pl.when(jnp.logical_not(down_x))(lambda: clear_sides(0))
     pl.when(jnp.logical_not(up_x))(lambda: clear_sides(1))
     for d in range(1, n_group):
@@ -90,29 +104,43 @@
             s_rrec[d - 1] = jnp.ones((cx, nz), jnp.float32)
             o_rrec[d - 1] = jnp.zeros((cx, nz), jnp.float32)
 
+    def remote(src, dst, send, recv, to):
+        return pltpu.make_async_remote_copy(
+            src_ref=src, dst_ref=dst, send_sem=send, recv_sem=recv, device_id=to, device_id_type=MESH)
+
     def halo_copies(st):
         f = fields[st]
         nf = f.shape[0]
-        plane = lambda y: f.at[:, (y + 1) * pitch:(y + 1) * pitch + nx]
-        parts = (
-            (up_y, down_y, plane(ny - 1), plane(-1), (ix, iy + 1)),
-            (down_y, up_y, plane(0), plane(ny), (ix, iy - 1)),
-            (up_x, down_x, xs.at[st, 1, :nf], xr.at[st, 0, :nf], (ix + 1, iy)),
-            (down_x, up_x, xs.at[st, 0, :nf], xr.at[st, 1, :nf], (ix - 1, iy)),
-        )
+        plane = lambda y: f.at[:, (y + 2) * pitch:(y + 2) * pitch + nx]
+        sides = (xs3, xr3) if st == 3 else (xs.at[st, :, :nf], xr.at[st, :, :nf])
+        parts = [
+            (up_x, down_x, sides[0].at[1], sides[1].at[0], (ix + 1, iy)),
+            (down_x, up_x, sides[0].at[0], sides[1].at[1], (ix - 1, iy)),
+        ]
+        if st < 3:
+            parts += [
+                (up_y, down_y, plane(ny - 1), plane(-1), (ix, iy + 1)),
+                (down_y, up_y, plane(0), plane(ny), (ix, iy - 1)),
+            ]
         return [
-            (sends, receives, pltpu.make_async_remote_copy(
-                src_ref=src, dst_ref=dst, send_sem=h_send.at[st, i], recv_sem=h_recv.at[st, i],
-                device_id=to, device_id_type=MESH))
+            (sends, receives, remote(src, dst, h_send.at[st, i], h_recv.at[st, i], to))
             for i, (sends, receives, src, dst, to) in enumerate(parts)
         ]
+
+    def side_rows(st, x):
+        more = 1 if st == 3 else 0
+        return pl.ds(first_on - more * pitch + x, ny + 2 * more, stride=pitch)
 
     def send_halo(st):
         f = fields[st]
         for n in range(f.shape[0]):
-            xs[st, 0, n] = f[n, pl.ds(pitch, ny, stride=pitch), :]
-            xs[st, 1, n] = f[n, pl.ds(pitch + nx - 1, ny, stride=pitch), :]
-        for sends, _, copy in halo_copies(st):
+            for side, x in ((0, 0), (1, nx - 1)):
+                if st == 3:
+                    xs3[side, n] = f[n, side_rows(st, x), :]
+                else:
+                    xs[st, side, n] = f[n, side_rows(st, x), :]
+        copies = halo_copies(st)
+        for sends, _, copy in copies[2:] + copies[:2]:
             pl.when(sends)(copy.start)
 
     def take_halo(st):
@@ -121,42 +149,73 @@
             pl.when(sends)(copy.wait_send)
             pl.when(receives)(copy.wait_recv)
         for n in range(f.shape[0]):
-            f[n, pl.ds(pitch - 1, ny, stride=pitch), :] = xr[st, 0, n]
-            f[n, pl.ds(pitch + nx, ny, stride=pitch), :] = xr[st, 1, n]
+            for side, x in ((0, -1), (1, nx)):
+                f[n, side_rows(st, x), :] = xr3[side, n] if st == 3 else xr[st, side, n]
+
+    def deep_copies(kind):
+        near = lambda ref, low, high: (ref.at[low:high] if len(ref.shape) == 2 else ref.at[:, low:high])
+        if kind == 0:
+            ups, downs = (cf, ny * nx, 0, nx), (cf, nx, (ny + 1) * nx, nx)
+        elif kind == 1:
+            ups = (fx, (ny + 1) * pitch - 8, pitch - 8, nx + 8)
+            downs = (fx, 2 * pitch - 8, (ny + 2) * pitch - 8, nx + 8)
+        elif kind == 2:
+            ups, downs = (fy, ny * nx, 0, nx), (fy, 2 * nx, (ny + 2) * nx, nx)
+        elif kind == 3:
+            ups, downs = (f2, ny * pitch, 0, nx), (f2, 3 * pitch, (ny + 3) * pitch, nx)
+        else:
+            ups, downs = (coarse, cy, 0, 1), (coarse, 1, cy + 1, 1)
+        return [
+            (sends, receives, remote(near(ref, src, src + n), near(ref, dst, dst + n),
+                                     w_send.at[kind, i], w_recv.at[kind, i], to))
+            for i, (sends, receives, to, (ref, src, dst, n)) in enumerate((
+                (up_y, down_y, (ix, iy + 1), ups), (down_y, up_y, (ix, iy - 1), downs)))
+        ]
+
+    def send_deep(*kinds):
+        for kind in kinds:
+            for sends, _, copy in deep_copies(kind):
+                pl.when(sends)(copy.start)
+
+    def take_deep(*kinds):
+        for kind in kinds:
+            for sends, receives, copy in deep_copies(kind):
+                pl.when(sends)(copy.wait_send)
+                pl.when(receives)(copy.wait_recv)
 
     def group_copies(kind, block, received):
         return [
-            pltpu.make_async_remote_copy(
-                src_ref=block, dst_ref=received.at[d - 1],
-                send_sem=g_send.at[kind, d - 1], recv_sem=g_recv.at[kind, d - 1],
-                device_id=(ix, row * group + lax.rem(place + d, group)), device_id_type=MESH)
+            remote(block, received.at[d - 1], g_send.at[kind, d - 1], g_recv.at[kind, d - 1],
+                   (ix, row * group + lax.rem(place + d, group)))
             for d in range(1, group)
         ]
 
     def row_copies(kind, block, received):
         return [
-            (row + d < n_group, row >= d, pltpu.make_async_remote_copy(
-                src_ref=block, dst_ref=received.at[d - 1],
-                send_sem=g_send.at[kind, d - 1], recv_sem=g_recv.at[kind, d - 1],
-                device_id=(ix, (row + d) * group + place), device_id_type=MESH))
+            (row + d < n_group, row >= d, remote(
+                block, received.at[d - 1], g_send.at[kind, d - 1], g_recv.at[kind, d - 1],
+                (ix, (row + d) * group + place)))
             for d in range(1, n_group)
         ]
 
     def plane(y):
-        return Cells(y * nx, (y + 1) * pitch, nx)
+        return Cells((y + 1) * nx, (y + 2) * pitch, nx)
 
     def inner(body, low=1, high=ny - 1, unroll=2):
         def step(y, _):
-            body(Cells(pl.multiple_of(y * nx, 8), pl.multiple_of((y + 1) * pitch, 8), nx))
+            body(Cells(pl.multiple_of((y + 1) * nx, 8), pl.multiple_of((y + 2) * pitch, 8), nx))
             return 0
 
         lax.fori_loop(low, high, step, 0, unroll=unroll)
 
+    def columns(body, more=0):
+        for x in (0, nx - 1):
+            body(Cells((1 - more) * nx + x, (2 - more) * pitch + x, ny + 2 * more, nx, pitch))
+
     def outer(body):
-        for y in (0, ny - 1):
-            body(plane(y))
-        for x in (0, nx - 1):
-            body(Cells(x, pitch + x, ny, nx, pitch))
+        body(plane(0))
+        body(plane(ny - 1))
+        columns(body)
 
     def conductivity(u):
         t = f0[0, u.field(), :]
@@ -175,18 +234,18 @@
         total = None
         for a in (0, step):
             for b in (0, 1):
-                part = load(pl.ds(2 * j * step + a + b, cx, stride=2))
+                part = load(2 * j * step + a + b)
                 total = part if total is None else total + part
         return total
 
     s_all = None
     for j in range(cy):
-        cs = block_sum(lambda at: c_f[at, :], j, nx)
-        cond = block_sum(lambda at: f0[2, pl.ds(at.start + pitch, at.size, stride=at.stride), :], j, pitch)
+        cs = block_sum(lambda at: c_f[pl.ds(nx + at, cx, stride=2), :], j, nx)
+        cond = block_sum(lambda at: f0[2, pl.ds(first_on + at, cx, stride=2), :], j, pitch)
         inv_solid = 1.0 / (4.0 * solid_cap + cs + lump_factor * cond)
         inv_denom = 1.0 / (4.0 * gas_cap + cs + 2.0 * flow_rate - cs * cs * inv_solid)
         slope = 2.0 * flow_rate * inv_denom
-        csum[j], isol[j], iden[j], slopes[j] = cs, inv_solid, inv_denom, slope
+        coarse[CSUM, j + 1], coarse[ISOL, j + 1], coarse[SLOPE, j + 1] = cs, inv_solid, slope
         s_all = slope if s_all is None else s_all * slope
     s_blk[...] = s_all
     for copy in group_copies(0, s_blk, s_rec):
@@ -213,27 +272,27 @@
             fx[u.field(-1), :] = xm
         fy[u.coef(), :] = ym
         fy[u.coef(nx), :] = yp
-        fz[u.coef(), :] = not_last * zp
+        cf[FZ, u.coef(), :] = not_last * zp
         k = c_f[u.coef(), :]
         sd = solid_cap + k + (((xp + xm) + (yp + ym)) + (zp + zm))
         gd = (gas_cap + flow_rate + gas_conduct * 2.0 * 2.25) + k
         w = relaxation / (sd * gd - k * k)
         diag[u.coef(), :] = sd
-        pp[u.coef(), :] = gd * w
-        qq[u.coef(), :] = k * w
-        rr[u.coef(), :] = sd * w
+        cf[P_, u.coef(), :] = gd * w
+        cf[Q_, u.coef(), :] = k * w
+        cf[R_, u.coef(), :] = sd * w
 
     def beside(f, u):
         s = f[0, u.field(), :]
         g = f[1, u.field(), :]
-        z = fz[u.coef(), :]
-        hs = b_f[0, u.coef(), :]
+        z = cf[FZ, u.coef(), :]
+        hs = cf[B_S, u.coef(), :]
         hs += fy[u.coef(nx), :] * f[0, u.field(pitch), :]
         hs += fy[u.coef(), :] * f[0, u.field(-pitch), :]
         hs += fx[u.field(), :] * f[0, u.field(1), :]
         hs += fx[u.field(-1), :] * f[0, u.field(-1), :]
         hs += z * pltpu.roll(s, nz - 1, 1) + pltpu.roll(z * s, 1, 1)
-        hg = b_f[1, u.coef(), :]
+        hg = cf[B_G, u.coef(), :]
         hg += (flow_rate + gas_conduct) * f[1, u.field(-pitch), :]
         hg += gas_conduct * (f[1, u.field(pitch), :] + (f[1, u.field(-1), :] + f[1, u.field(1), :]))
         hg += gas_zp * pltpu.roll(g, nz - 1, 1) + gas_zm * pltpu.roll(g, 1, 1)
@@ -241,7 +300,7 @@
 
     def relaxed(f, u):
         s, g, hs, hg = beside(f, u)
-        p, q, r = pp[u.coef(), :], qq[u.coef(), :], rr[u.coef(), :]
+        p, q, r = (cf[n, u.coef(), :] for n in (P_, Q_, R_))
         keep = 1.0 - relaxation
         return keep * s + (p * hs + q * hg), keep * g + (q * hs + r * hg)
 
@@ -257,6 +316,7 @@
     outer(set_up)
     outer(sweep(f0, f1))
     send_halo(1)
+    send_deep(0, 1, 2)
     inner(sweep(f1, f2))
 
     def upstream(d):
@@ -277,6 +337,7 @@
     take_halo(1)
     outer(sweep(f1, f2))
     send_halo(2)
+    send_deep(3)
 
     def residual(u):
         s, g, hs, hg = beside(f2, u)
@@ -291,14 +352,16 @@
 
     state = jnp.zeros((cx, nz), jnp.float32)
     for j in range(cy):
-        r_s = block_sum(lambda at: res[0, at, :], j, nx)
-        r_g = block_sum(lambda at: res[1, at, :], j, nx)
-        offset = (r_g + csum[j] * r_s * isol[j]) * iden[j]
-        cres[j], offs[j] = r_s, offset
-        state = slopes[j] * state + offset
+        r_s = block_sum(lambda at: res[0, pl.ds(nx + at, cx, stride=2), :], j, nx)
+        r_g = block_sum(lambda at: res[1, pl.ds(nx + at, cx, stride=2), :], j, nx)
+        slope = coarse[SLOPE, j + 1]
+        offset = (r_g + coarse[CSUM, j + 1] * r_s * coarse[ISOL, j + 1]) * (slope * (0.5 / flow_rate))
+        coarse[CRES, j + 1], coarse[OFFS, j + 1] = r_s, offset
+        state = slope * state + offset
     o_blk[...] = state
     for copy in group_copies(2, o_blk, o_rec):
         copy.start()
+    send_deep(4)
     for sends, receives, copy in row_copies(1, s_row, s_rrec):
         pl.when(sends)(copy.wait_send)
         pl.when(receives)(copy.wait_recv)
@@ -321,12 +384,14 @@
     for d in range(n_group - 1, 0, -1):
         state = s_rrec[d - 1] * state + o_rrec[d - 1]
     error = s_pre[...] * state + before
-    for j in range(cy):
-        error = slopes[j] * error + offs[j]
-        solid_error = (cres[j] + csum[j] * error) * isol[j]
-        for a in (pitch, 2 * pitch):
+    take_deep(0, 1, 2, 3, 4)
+    for j in range(-1, cy + 1):
+        if j >= 0:
+            error = coarse[SLOPE, j + 1] * error + coarse[OFFS, j + 1]
+        solid_error = (coarse[CRES, j + 1] + coarse[CSUM, j + 1] * error) * coarse[ISOL, j + 1]
+        for y in (2 * j, 2 * j + 1):
             for b in (0, 1):
-                at = pl.ds(2 * j * pitch + a + b, cx, stride=2)
+                at = pl.ds((y + 2) * pitch + b, cx, stride=2)
                 f3[0, at, :] = f2[0, at, :] + solid_error
                 f3[1, at, :] = f2[1, at, :] + error
 
@@ -334,14 +399,14 @@
         o_v[0, u.coef(), :], o_v[1, u.coef(), :] = relaxed(f4, u)
 
     send_halo(3)
-    inner(sweep(f3, f4))
+    inner(sweep(f3, f4), -1, ny + 1)
     take_halo(3)
-    outer(sweep(f3, f4))
+    columns(sweep(f3, f4), 1)
     send_halo(4)
-    inner(last)
+    inner(last, 0, ny)
     take_halo(4)
-    outer(last)
-    store = pltpu.make_async_copy(o_v, out, in_sem.at[0])
+    columns(last)
+    store = pltpu.make_async_copy(o_v.at[:, own], out, in_sem.at[0])
     store.start()
     store.wait()
 
@@ -352,21 +417,22 @@
     n_group = n_gy // group
     rows, cx, cy = nx * ny, nx // 2, ny // 2
     f32 = jnp.float32
-    padded = (nx + EDGE) * (ny + 2)
+    padded = (nx + EDGE) * (ny + 4)
+    ext = rows + 2 * nx
     kinds = max(group, n_group) - 1
     vmem = lambda *shape: pltpu.VMEM(shape, f32)
     line = lambda *lead: pltpu.VMEM((*lead, cx, nz), f32)
     scratch = [
-        vmem(rows, nz), vmem(2, rows, nz), vmem(rows, nz), vmem(2, rows, nz),
+        vmem(ext, nz), vmem(ext, nz), vmem(2, ext, nz),
         vmem(3, padded, nz), vmem(2, padded, nz), vmem(2, padded, nz), vmem(2, padded, nz), vmem(2, padded, nz),
-        vmem(padded, nz), vmem(rows + nx, nz), vmem(rows, nz), vmem(rows, nz),
-        vmem(rows, nz), vmem(rows, nz), vmem(rows, nz), vmem(2, rows, nz),
-        vmem(STAGES, 2, 3, ny, nz), vmem(STAGES, 2, 3, ny, nz),
-        line(cy), line(cy), line(cy), line(cy), line(cy), line(cy),
+        vmem(6, ext, nz), vmem(padded, nz), vmem(ext + nx, nz), vmem(ext, nz), vmem(2, ext, nz),
+        vmem(STAGES, 2, 3, ny, nz), vmem(STAGES, 2, 3, ny, nz), vmem(2, 2, ny + 2, nz), vmem(2, 2, ny + 2, nz),
+        line(5, cy + 2),
         line(), line(), line(group - 1), line(group - 1),
         line(), line(), line(n_group - 1), line(n_group - 1), line(),
         pltpu.SemaphoreType.DMA((3 + ny,)),
         pltpu.SemaphoreType.DMA((STAGES, 4)), pltpu.SemaphoreType.DMA((STAGES, 4)),
+        pltpu.SemaphoreType.DMA((5, 2)), pltpu.SemaphoreType.DMA((5, 2)),
         pltpu.SemaphoreType.DMA((4, kinds)), pltpu.SemaphoreType.DMA((4, kinds)),
     ]
     flat = lambda a: jnp.swapaxes(a, -3, -2).reshape(*a.shape[:-3], rows, nz)

time: 42.9 us -> 41.3 us (0.963)
  Pallas kernels: 41 us -> 39.3 us
    pallas_call x1, Pallas kernels: 41 us -> 39.3 us  [shards(): pl.pallas_call(functools.partial(kernel, (nx, ny, nz, n_gx, n_gy, group))...]
where the time goes in v4:
time: 41.3 us; the launch traced here: 41.1 us
  Pallas kernels  39.3 us (95%)
  local copies, waits for them, and re-layouts  1.77 us (4%)
    pallas_call x1, Pallas kernels, shards(): pl.pallas_call(functools.partial(kernel, (nx, ny, nz, n_gx, n_gy, group))...  39.3 us
    unnamed x1, local copies, waits for them, and re-layouts  1.77 us

profile of v4, /device:TPU:56, one launch (start us, length us, event | category | flops | bytes accessed | tf_op | source)
XLA Modules:
  0.0 41.1 jit_solution(13568026338330530378)
XLA Ops:
  0.0 39.3 %shard_map.46 = f32[2,384,128]{2,1,0:T(8,128)} custom-call(f32[2,384,128]{2,1,0:T(8,128)} %bitcast.16, f32[2,384,128]{2,1,0:T(8,128)} %bitcast.17, f32[384,128]{1,0:T(8,128)} %bitcast.18, f32[384,128]{1,0:T(8,128)} %bitcast.19), custom_call_target="tpu_custom_call" | custom-call | tf_op jit(solution)/shard_map/pallas_call | solution.py:439
  39.3 1.8 %copy.6 = f32[2,32,12,128]{3,1,2,0:T(8,128)} copy(f32[2,32,12,128]{3,1,2,0:T(8,128)} %bitcast.15) | data formatting | bytes 786432

commit v5 on v4

--- a/solution.py
+++ b/solution.py
@@ -16,7 +16,7 @@
 gas_conduct = 0.05
 relaxation = 0.8
 lump_factor = 0.25
-STAGES = 5
+STAGES = 4
 
 
 class Cells:
@@ -35,12 +35,12 @@
     pitch = nx + EDGE
     cx, cy = nx // 2, ny // 2
     n_group = n_gy // group
-    (e_in, c_f, o_v, f0, f1, f2, f3, f4, cf, fx, fy, diag, res, xs, xr, xs3, xr3, coarse,
+    (e_in, c_f, o_v, f0, f1, f2, f3, f4, cf, fx, fy, diag, res, xs, xr, xs3, xr3, cs3, cr3, coarse,
      s_blk, o_blk, s_rec, o_rec, s_row, o_row, s_rrec, o_rrec, s_pre,
      in_sem, h_send, h_recv, w_send, w_recv, g_send, g_recv) = scratch
     P_, Q_, R_, FZ, B_S, B_G = range(6)
     CSUM, ISOL, CRES, SLOPE, OFFS = range(5)
-    own = slice(nx, (ny + 1) * nx)
+    mine = slice(nx, (ny + 1) * nx)
     first_on = 2 * pitch
     ix, iy = lax.axis_index("gx"), lax.axis_index("gy")
     place, row = lax.rem(iy, group), lax.div(iy, group)
@@ -49,8 +49,8 @@
         pltpu.make_async_copy(temps.at[:, pl.ds(y * nx, nx)], f0.at[0:2, pl.ds((y + 2) * pitch, nx)], in_sem.at[3 + y])
         for y in range(ny)
     ]
-    loads.append(pltpu.make_async_copy(exch, e_in.at[own], in_sem.at[0]))
-    more = [pltpu.make_async_copy(coup, c_f.at[own], in_sem.at[1]), pltpu.make_async_copy(right, cf.at[B_S:B_G + 1, own], in_sem.at[2])]
+    loads.append(pltpu.make_async_copy(exch, e_in.at[mine], in_sem.at[0]))
+    more = [pltpu.make_async_copy(coup, c_f.at[mine], in_sem.at[1]), pltpu.make_async_copy(right, cf.at[B_S:B_G + 1, mine], in_sem.at[2])]
     for load in loads + more:
         load.start()
 
@@ -90,8 +90,10 @@
         for st in range(STAGES):
             for n in range(3 if st == 0 else 2):
                 xr[st, side, n] = side_zero
-        for n in range(2):
+        for n in range(4):
             xr3[side, n] = jnp.zeros((ny + 2, nz), jnp.float32)
+        for n in range(10):
+            cr3[side, n] = side_zero
 
     pl.when(jnp.logical_not(down_y))(lambda: clear_planes(-1, -2, 0, 0))
     pl.when(jnp.logical_not(up_y))(lambda: clear_planes(ny, ny + 1, ny + 2, cy + 1))
@@ -134,9 +136,10 @@
     def send_halo(st):
         f = fields[st]
         for n in range(f.shape[0]):
-            for side, x in ((0, 0), (1, nx - 1)):
+            for side, x, deeper in ((0, 0, 1), (1, nx - 1, nx - 2)):
                 if st == 3:
                     xs3[side, n] = f[n, side_rows(st, x), :]
+                    xs3[side, 2 + n] = f[n, side_rows(st, deeper), :]
                 else:
                     xs[st, side, n] = f[n, side_rows(st, x), :]
         copies = halo_copies(st)
@@ -149,10 +152,19 @@
             pl.when(sends)(copy.wait_send)
             pl.when(receives)(copy.wait_recv)
         for n in range(f.shape[0]):
-            for side, x in ((0, -1), (1, nx)):
-                f[n, side_rows(st, x), :] = xr3[side, n] if st == 3 else xr[st, side, n]
+            for side, x, deeper in ((0, -1, -2), (1, nx, nx + 1)):
+                if st == 3:
+                    f[n, side_rows(st, x), :] = xr3[side, n]
+                    f[n, side_rows(st, deeper), :] = xr3[side, 2 + n]
+                else:
+                    f[n, side_rows(st, x), :] = xr[st, side, n]
 
     def deep_copies(kind):
+        if kind == 5:
+            return [
+                (up_x, down_x, remote(cs3.at[1], cr3.at[0], w_send.at[5, 0], w_recv.at[5, 0], (ix + 1, iy))),
+                (down_x, up_x, remote(cs3.at[0], cr3.at[1], w_send.at[5, 1], w_recv.at[5, 1], (ix - 1, iy))),
+            ]
         near = lambda ref, low, high: (ref.at[low:high] if len(ref.shape) == 2 else ref.at[:, low:high])
         if kind == 0:
             ups, downs = (cf, ny * nx, 0, nx), (cf, nx, (ny + 1) * nx, nx)
@@ -208,8 +220,8 @@
 
         lax.fori_loop(low, high, step, 0, unroll=unroll)
 
-    def columns(body, more=0):
-        for x in (0, nx - 1):
+    def columns(body, more=0, at=(0, nx - 1)):
+        for x in at:
             body(Cells((1 - more) * nx + x, (2 - more) * pitch + x, ny + 2 * more, nx, pitch))
 
     def outer(body):
@@ -282,17 +294,39 @@
         cf[Q_, u.coef(), :] = k * w
         cf[R_, u.coef(), :] = sd * w
 
+    class Given:
+        def __init__(self, x, side):
+            self.on, self.side = first_on + x, side
+
+        def field(self, shift=0):
+            return pl.ds(self.on + shift, ny, stride=pitch)
+
+        def own(self, n):
+            return cr3[self.side, n]
+
+        def faces(self):
+            return tuple(cr3[self.side, n] for n in (6, 7, 8, 9))
+
+    def own(u, n):
+        return u.own(n) if isinstance(u, Given) else cf[n, u.coef(), :]
+
+    def faces(u):
+        if isinstance(u, Given):
+            return u.faces()
+        return fx[u.field(-1), :], fx[u.field(), :], fy[u.coef(), :], fy[u.coef(nx), :]
+
     def beside(f, u):
         s = f[0, u.field(), :]
         g = f[1, u.field(), :]
-        z = cf[FZ, u.coef(), :]
-        hs = cf[B_S, u.coef(), :]
-        hs += fy[u.coef(nx), :] * f[0, u.field(pitch), :]
-        hs += fy[u.coef(), :] * f[0, u.field(-pitch), :]
-        hs += fx[u.field(), :] * f[0, u.field(1), :]
-        hs += fx[u.field(-1), :] * f[0, u.field(-1), :]
+        z = own(u, FZ)
+        xm, xp, ym, yp = faces(u)
+        hs = own(u, B_S)
+        hs += yp * f[0, u.field(pitch), :]
+        hs += ym * f[0, u.field(-pitch), :]
+        hs += xp * f[0, u.field(1), :]
+        hs += xm * f[0, u.field(-1), :]
         hs += z * pltpu.roll(s, nz - 1, 1) + pltpu.roll(z * s, 1, 1)
-        hg = cf[B_G, u.coef(), :]
+        hg = own(u, B_G)
         hg += (flow_rate + gas_conduct) * f[1, u.field(-pitch), :]
         hg += gas_conduct * (f[1, u.field(pitch), :] + (f[1, u.field(-1), :] + f[1, u.field(1), :]))
         hg += gas_zp * pltpu.roll(g, nz - 1, 1) + gas_zm * pltpu.roll(g, 1, 1)
@@ -300,7 +334,7 @@
 
     def relaxed(f, u):
         s, g, hs, hg = beside(f, u)
-        p, q, r = (cf[n, u.coef(), :] for n in (P_, Q_, R_))
+        p, q, r = own(u, P_), own(u, Q_), own(u, R_)
         keep = 1.0 - relaxation
         return keep * s + (p * hs + q * hg), keep * g + (q * hs + r * hg)
 
@@ -316,7 +350,13 @@
     outer(set_up)
     outer(sweep(f0, f1))
     send_halo(1)
-    send_deep(0, 1, 2)
+    for side, x in ((0, 0), (1, nx - 1)):
+        u = Cells(nx + x, first_on + x, ny, nx, pitch)
+        for n in range(6):
+            cs3[side, n] = cf[n, u.coef(), :]
+        cs3[side, 6], cs3[side, 7] = fx[u.field(-1), :], fx[u.field(), :]
+        cs3[side, 8], cs3[side, 9] = fy[u.coef(), :], fy[u.coef(nx), :]
+    send_deep(0, 1, 2, 5)
     inner(sweep(f1, f2))
 
     def upstream(d):
@@ -384,7 +424,7 @@
     for d in range(n_group - 1, 0, -1):
         state = s_rrec[d - 1] * state + o_rrec[d - 1]
     error = s_pre[...] * state + before
-    take_deep(0, 1, 2, 3, 4)
+    take_deep(0, 1, 2, 3, 4, 5)
     for j in range(-1, cy + 1):
         if j >= 0:
             error = coarse[SLOPE, j + 1] * error + coarse[OFFS, j + 1]
@@ -400,13 +440,13 @@
 
     send_halo(3)
     inner(sweep(f3, f4), -1, ny + 1)
+    inner(last, 0, ny)
     take_halo(3)
     columns(sweep(f3, f4), 1)
-    send_halo(4)
-    inner(last, 0, ny)
-    take_halo(4)
-    columns(last)
-    store = pltpu.make_async_copy(o_v.at[:, own], out, in_sem.at[0])
+    sweep(f3, f4)(Given(-1, 0))
+    sweep(f3, f4)(Given(nx, 1))
+    columns(last, 0, (0, 1, nx - 2, nx - 1))
+    store = pltpu.make_async_copy(o_v.at[:, mine], out, in_sem.at[0])
     store.start()
     store.wait()
 
@@ -426,13 +466,13 @@
         vmem(ext, nz), vmem(ext, nz), vmem(2, ext, nz),
         vmem(3, padded, nz), vmem(2, padded, nz), vmem(2, padded, nz), vmem(2, padded, nz), vmem(2, padded, nz),
         vmem(6, ext, nz), vmem(padded, nz), vmem(ext + nx, nz), vmem(ext, nz), vmem(2, ext, nz),
-        vmem(STAGES, 2, 3, ny, nz), vmem(STAGES, 2, 3, ny, nz), vmem(2, 2, ny + 2, nz), vmem(2, 2, ny + 2, nz),
+        vmem(STAGES, 2, 3, ny, nz), vmem(STAGES, 2, 3, ny, nz), vmem(2, 4, ny + 2, nz), vmem(2, 4, ny + 2, nz), vmem(2, 10, ny, nz), vmem(2, 10, ny, nz),
         line(5, cy + 2),
         line(), line(), line(group - 1), line(group - 1),
         line(), line(), line(n_group - 1), line(n_group - 1), line(),
         pltpu.SemaphoreType.DMA((3 + ny,)),
         pltpu.SemaphoreType.DMA((STAGES, 4)), pltpu.SemaphoreType.DMA((STAGES, 4)),
-        pltpu.SemaphoreType.DMA((5, 2)), pltpu.SemaphoreType.DMA((5, 2)),
+        pltpu.SemaphoreType.DMA((6, 2)), pltpu.SemaphoreType.DMA((6, 2)),
         pltpu.SemaphoreType.DMA((4, kinds)), pltpu.SemaphoreType.DMA((4, kinds)),
     ]
     flat = lambda a: jnp.swapaxes(a, -3, -2).reshape(*a.shape[:-3], rows, nz)

time: 41.3 us -> 37.6 us (0.910)
  Pallas kernels: 39.3 us -> 35.6 us
    pallas_call x1, Pallas kernels: 39.3 us -> 35.6 us  [shards(): pl.pallas_call(functools.partial(kernel, (nx, ny, nz, n_gx, n_gy, group))...]
where the time goes in v5:
time: 37.6 us; the launch traced here: 37.4 us
  Pallas kernels  35.6 us (95%)
  local copies, waits for them, and re-layouts  1.77 us (5%)
    pallas_call x1, Pallas kernels, shards(): pl.pallas_call(functools.partial(kernel, (nx, ny, nz, n_gx, n_gy, group))...  35.6 us
    unnamed x1, local copies, waits for them, and re-layouts  1.77 us

profile of v5, /device:TPU:56, one launch (start us, length us, event | category | flops | bytes accessed | tf_op | source)
XLA Modules:
  0.0 37.4 jit_solution(4395606999974084133)
XLA Ops:
  0.0 35.6 %shard_map.46 = f32[2,384,128]{2,1,0:T(8,128)} custom-call(f32[2,384,128]{2,1,0:T(8,128)} %bitcast.16, f32[2,384,128]{2,1,0:T(8,128)} %bitcast.17, f32[384,128]{1,0:T(8,128)} %bitcast.18, f32[384,128]{1,0:T(8,128)} %bitcast.19), custom_call_target="tpu_custom_call" | custom-call | tf_op jit(solution)/shard_map/pallas_call | solution.py:479
  35.6 1.8 %copy.6 = f32[2,32,12,128]{3,1,2,0:T(8,128)} copy(f32[2,32,12,128]{3,1,2,0:T(8,128)} %bitcast.15) | data formatting | bytes 786432

commit v6 on v5

--- a/solution.py
+++ b/solution.py
@@ -17,6 +17,7 @@
 relaxation = 0.8
 lump_factor = 0.25
 STAGES = 4
+REACH = 2
 
 
 class Cells:
@@ -37,7 +38,7 @@
     n_group = n_gy // group
     (e_in, c_f, o_v, f0, f1, f2, f3, f4, cf, fx, fy, diag, res, xs, xr, xs3, xr3, cs3, cr3, coarse,
      s_blk, o_blk, s_rec, o_rec, s_row, o_row, s_rrec, o_rrec, s_pre,
-     in_sem, h_send, h_recv, w_send, w_recv, g_send, g_recv) = scratch
+     news, in_sem, h_send, h_recv, w_send, w_recv, g_send, g_recv) = scratch
     P_, Q_, R_, FZ, B_S, B_G = range(6)
     CSUM, ISOL, CRES, SLOPE, OFFS = range(5)
     mine = slice(nx, (ny + 1) * nx)
@@ -61,8 +62,10 @@
 
     for d in range(1, group):
         greet(ix, row * group + lax.rem(place + d, group))
-    for d in range(1, n_group):
-        greet(ix, lax.rem(row + d, n_group) * group + place)
+    near_rows = [(row + d < n_group, row + d) for d in range(1, min(REACH, n_group - 1) + 1)]
+    near_rows += [(row >= d, row - d) for d in range(1, min(REACH, n_group - 1) + 1)]
+    for there, other in near_rows:
+        pl.when(there)(lambda other=other: greet(ix, other * group + place))
     up_y, down_y, up_x, down_x = iy < n_gy - 1, iy > 0, ix < n_gx - 1, ix > 0
     pl.when(up_y)(lambda: greet(ix, iy + 1))
     pl.when(down_y)(lambda: greet(ix, iy - 1))
@@ -236,9 +239,25 @@
     for load in loads:
         load.wait()
     inner(conductivity, 0, ny)
-    n_halo = sum(v.astype(jnp.int32) for v in (up_y, down_y, up_x, down_x))
-    pl.semaphore_wait(barrier, (group - 1) + (n_group - 1) + n_halo)
+    n_some = sum(v.astype(jnp.int32) for v in (up_y, down_y, up_x, down_x, *(there for there, _ in near_rows)))
+    pl.semaphore_wait(barrier, group - 1 + n_some)
     send_halo(0)
+
+    rounds = max(0, -(-(n_group - 1 - REACH) // REACH))
+
+    def tell(k):
+        if k < rounds:
+
+            @pl.when(row >= REACH)
+            def _():
+                pl.semaphore_signal(
+                    news.at[k], inc=1, device_id=(ix, (row - REACH) * group + place), device_id_type=MESH)
+
+    def hear(k):
+        if k < rounds:
+            pl.when(row + REACH < n_group)(lambda: pl.semaphore_wait(news.at[k], 1))
+
+    tell(0)
     for load in more:
         load.wait()
 
@@ -346,6 +365,8 @@
 
     inner(set_up)
     inner(sweep(f0, f1))
+    hear(0)
+    tell(1)
     take_halo(0)
     outer(set_up)
     outer(sweep(f0, f1))
@@ -371,8 +392,8 @@
         s_after = jnp.where(upstream(d), s_after, s_after * s_d)
     s_pre[...] = s_before
     s_row[...] = s_before * s_blk[...] * s_after
-    for sends, _, copy in row_copies(1, s_row, s_rrec):
-        pl.when(sends)(copy.start)
+    hear(1)
+    tell(2)
 
     take_halo(1)
     outer(sweep(f1, f2))
@@ -387,6 +408,11 @@
         res[1, u.coef(), :] = hg - (gd * g - k * s)
 
     inner(residual)
+    for k in range(2, rounds):
+        hear(k)
+        tell(k + 1)
+    for sends, _, copy in row_copies(1, s_row, s_rrec):
+        pl.when(sends)(copy.start)
     take_halo(2)
     outer(residual)
 
@@ -470,7 +496,7 @@
         line(5, cy + 2),
         line(), line(), line(group - 1), line(group - 1),
         line(), line(), line(n_group - 1), line(n_group - 1), line(),
-        pltpu.SemaphoreType.DMA((3 + ny,)),
+        pltpu.SemaphoreType.REGULAR((8,)), pltpu.SemaphoreType.DMA((3 + ny,)),
         pltpu.SemaphoreType.DMA((STAGES, 4)), pltpu.SemaphoreType.DMA((STAGES, 4)),
         pltpu.SemaphoreType.DMA((6, 2)), pltpu.SemaphoreType.DMA((6, 2)),
         pltpu.SemaphoreType.DMA((4, kinds)), pltpu.SemaphoreType.DMA((4, kinds)),

time: 37.6 us -> 36 us (0.957)
  Pallas kernels: 35.6 us -> 33.8 us
    pallas_call x1, Pallas kernels: 35.6 us -> 33.8 us  [shards(): pl.pallas_call(functools.partial(kernel, (nx, ny, nz, n_gx, n_gy, group))...]
where the time goes in v6:
time: 36 us; the launch traced here: 35.5 us
  Pallas kernels  33.8 us (94%)
  local copies, waits for them, and re-layouts  1.77 us (5%)
    pallas_call x1, Pallas kernels, shards(): pl.pallas_call(functools.partial(kernel, (nx, ny, nz, n_gx, n_gy, group))...  33.8 us
    unnamed x1, local copies, waits for them, and re-layouts  1.77 us

profile of v6, /device:TPU:56, one launch (start us, length us, event | category | flops | bytes accessed | tf_op | source)
XLA Modules:
  0.0 35.5 jit_solution(5678970579208772705)
XLA Ops:
  0.0 33.8 %shard_map.46 = f32[2,384,128]{2,1,0:T(8,128)} custom-call(f32[2,384,128]{2,1,0:T(8,128)} %bitcast.16, f32[2,384,128]{2,1,0:T(8,128)} %bitcast.17, f32[384,128]{1,0:T(8,128)} %bitcast.18, f32[384,128]{1,0:T(8,128)} %bitcast.19), custom_call_target="tpu_custom_call" | custom-call | tf_op jit(solution)/shard_map/pallas_call | solution.py:505
  33.8 1.8 %copy.6 = f32[2,32,12,128]{3,1,2,0:T(8,128)} copy(f32[2,32,12,128]{3,1,2,0:T(8,128)} %bitcast.15) | data formatting | bytes 786432

commit v7 on v6

--- a/solution.py
+++ b/solution.py
@@ -36,7 +36,7 @@
     pitch = nx + EDGE
     cx, cy = nx // 2, ny // 2
     n_group = n_gy // group
-    (e_in, c_f, o_v, f0, f1, f2, f3, f4, cf, fx, fy, diag, res, xs, xr, xs3, xr3, cs3, cr3, coarse,
+    (e_in, c_f, f0, f1, f2, f3, f4, cf, fx, fy, diag, res, xs, xr, xs3, xr3, cs3, cr3, coarse,
      s_blk, o_blk, s_rec, o_rec, s_row, o_row, s_rrec, o_rrec, s_pre,
      news, in_sem, h_send, h_recv, w_send, w_recv, g_send, g_recv) = scratch
     P_, Q_, R_, FZ, B_S, B_G = range(6)
@@ -462,7 +462,7 @@
                 f3[1, at, :] = f2[1, at, :] + error
 
     def last(u):
-        o_v[0, u.coef(), :], o_v[1, u.coef(), :] = relaxed(f4, u)
+        out[0, u.coef(-nx), :], out[1, u.coef(-nx), :] = relaxed(f4, u)
 
     send_halo(3)
     inner(sweep(f3, f4), -1, ny + 1)
@@ -472,9 +472,6 @@
     sweep(f3, f4)(Given(-1, 0))
     sweep(f3, f4)(Given(nx, 1))
     columns(last, 0, (0, 1, nx - 2, nx - 1))
-    store = pltpu.make_async_copy(o_v.at[:, mine], out, in_sem.at[0])
-    store.start()
-    store.wait()
 
 
 def shards(n_gx, n_gy, temps, right_side, exchange, coupling):
@@ -489,7 +486,7 @@
     vmem = lambda *shape: pltpu.VMEM(shape, f32)
     line = lambda *lead: pltpu.VMEM((*lead, cx, nz), f32)
     scratch = [
-        vmem(ext, nz), vmem(ext, nz), vmem(2, ext, nz),
+        vmem(ext, nz), vmem(ext, nz),
         vmem(3, padded, nz), vmem(2, padded, nz), vmem(2, padded, nz), vmem(2, padded, nz), vmem(2, padded, nz),
         vmem(6, ext, nz), vmem(padded, nz), vmem(ext + nx, nz), vmem(ext, nz), vmem(2, ext, nz),
         vmem(STAGES, 2, 3, ny, nz), vmem(STAGES, 2, 3, ny, nz), vmem(2, 4, ny + 2, nz), vmem(2, 4, ny + 2, nz), vmem(2, 10, ny, nz), vmem(2, 10, ny, nz),
@@ -504,9 +501,9 @@
     flat = lambda a: jnp.swapaxes(a, -3, -2).reshape(*a.shape[:-3], rows, nz)
     out = pl.pallas_call(
         functools.partial(kernel, (nx, ny, nz, n_gx, n_gy, group)),
-        out_shape=jax.ShapeDtypeStruct((2, rows, nz), f32),
+        out_shape=pltpu.VMEM((2, rows, nz), f32),
         in_specs=[pl.BlockSpec(memory_space=pl.ANY)] * 4,
-        out_specs=pl.BlockSpec(memory_space=pl.ANY),
+        out_specs=pl.BlockSpec(memory_space=pltpu.VMEM),
         scratch_shapes=scratch,
         compiler_params=pltpu.CompilerParams(collective_id=0, has_side_effects=True),
     )(flat(temps), flat(right_side), flat(exchange), flat(coupling))

time: 36 us -> 34.2 us (0.950)
  local copies, waits for them, and re-layouts: 1.77 us -> 0.75 us
  Pallas kernels: 33.8 us -> 33 us
    unnamed x1, local copies, waits for them, and re-layouts: 1.77 us -> 0.75 us
    pallas_call x1, Pallas kernels: 33.8 us -> 33 us  [shards(): pl.pallas_call(functools.partial(kernel, (nx, ny, nz, n_gx, n_gy, group))...]
where the time goes in v7:
time: 34.2 us; the launch traced here: 33.8 us
  Pallas kernels  33 us (96%)
  local copies, waits for them, and re-layouts  0.75 us (2%)
    pallas_call x1, Pallas kernels, shards(): pl.pallas_call(functools.partial(kernel, (nx, ny, nz, n_gx, n_gy, group))...  33 us
    unnamed x1, local copies, waits for them, and re-layouts  0.75 us

profile of v7, /device:TPU:56, one launch (start us, length us, event | category | flops | bytes accessed | tf_op | source)
XLA Modules:
  0.0 33.8 jit_solution(15911980465234067429)
XLA Ops:
  0.0 33.0 %shard_map.46 = f32[2,384,128]{2,1,0:T(8,128)S(1)} custom-call(f32[2,384,128]{2,1,0:T(8,128)} %bitcast.16, f32[2,384,128]{2,1,0:T(8,128)} %bitcast.17, f32[384,128]{1,0:T(8,128)} %bitcast.18, f32[384,128]{1,0:T(8,128)} %bitcast.19), custom_call_target="tpu_custom_call" | custom-call | tf_op jit(solution)/shard_map/pallas_call | solution.py:502
  33.0 0.7 %copy.6 = f32[2,32,12,128]{3,1,2,0:T(8,128)} copy(f32[2,32,12,128]{3,1,2,0:T(8,128)S(1)} %bitcast.15) | data formatting | bytes 786432
